TPU v7x, 128 devices: a whole 4x4x4 slice. The times are simulated.
128 devices in a mesh: rep: 4 (over y), shard: 32 (over x, z, core).
Axes of the slice: x: 4, y: 4, z: 4, core: 2. Of those that a mesh axis runs over, the one named last changes fastest.
Arguments:
- short_tokens: bfloat16 [256, 64, 768], P(('rep', 'shard')), may hold values from -6 to 6
- long_tokens: bfloat16 [256, 256, 768], P(('rep', 'shard')), may hold values from -6 to 6
- short_lengths: int32 [256], P(('rep', 'shard')), may hold values from 16 to 64
- long_lengths: int32 [256], P(('rep', 'shard')), may hold values from 65 to 256
- short_cotangent: bfloat16 [256, 64, 768], P(('rep', 'shard')), may hold values from -6 to 6
- long_cotangent: bfloat16 [256, 256, 768], P(('rep', 'shard')), may hold values from -6 to 6
- input_weight: bfloat16 [768, 2304], P('shard'), may hold values from -0.21875 to 0.21875
- query_bias: bfloat16 [768], P('shard'), may hold values from -3 to 3
- value_bias: bfloat16 [768], P('shard'), may hold values from -1.1953125 to 1.1953125
- output_weight: bfloat16 [768, 768], P('shard'), may hold values from -0.625 to 0.625
- output_bias: bfloat16 [768], P('shard'), may hold values from -1.1953125 to 1.1953125
- first_gain: bfloat16 [768], P('shard'), may hold values from 0.5 to 1.5
- first_shift: bfloat16 [768], P('shard'), may hold values from -1.1953125 to 1.1953125
- up_weight: bfloat16 [768, 3072], P('shard'), may hold values from -0.21875 to 0.21875
- up_bias: bfloat16 [3072], P('shard'), may hold values from -3 to 3
- down_weight: bfloat16 [3072, 768], P('shard'), may hold values from -0.109375 to 0.109375
- down_bias: bfloat16 [768], P('shard'), may hold values from -1.1953125 to 1.1953125
- second_gain: bfloat16 [768], P('shard'), may hold values from 0.5 to 1.5
- second_shift: bfloat16 [768], P('shard'), may hold values from -1.1953125 to 1.1953125
Outputs:
- short_out: bfloat16 [256, 64, 768], P(('rep', 'shard'))
- long_out: bfloat16 [256, 256, 768], P(('rep', 'shard'))
- short_grad: float32 [256, 64, 768], P(('rep', 'shard'))
- long_grad: float32 [256, 256, 768], P(('rep', 'shard'))
- grad_input_weight: float32 [768, 2304], P('shard')
- grad_query_bias: float32 [768], P('shard')
- grad_value_bias: float32 [768], P('shard')
- grad_output_weight: float32 [768, 768], P('shard')
- grad_output_bias: float32 [768], P('shard')
- grad_first_gain: float32 [768], P('shard')
- grad_first_shift: float32 [768], P('shard')
- grad_up_weight: float32 [768, 3072], P('shard')
- grad_up_bias: float32 [3072], P('shard')
- grad_down_weight: float32 [3072, 768], P('shard')
- grad_down_bias: float32 [768], P('shard')
- grad_second_gain: float32 [768], P('shard')
- grad_second_shift: float32 [768], P('shard')
All inputs are finite; a program needn't handle non-finite values.
Results may differ from a plain program's by a relative error of at most 0.025.
Values may be sent and summed in bfloat16 or wider, within the bound.
No kernel may reach another device: no remote copies, remote signals or barrier semaphores. Data moves between devices by JAX's collectives and lax.ppermute only.
A program may use at most 192 MiB of HBM per device.

v0:
```python
import math

import jax
import jax.numpy as jnp
from jax import lax
from jax.sharding import PartitionSpec as P

HEAD_DIM = 64


EPSILON = 1e-06


def in_one_piece(arrays, axis, dim, along):
    columns = [a.reshape(*a.shape[:along], -1) for a in arrays]
    both = jnp.concatenate(columns, axis=along)
    whole, at, done = (lax.all_gather(both, axis, axis=dim, tiled=True), 0, [])
    for a, column in zip(arrays, columns):
        share = whole[..., at : at + column.shape[along]]
        done.append(share.reshape(*share.shape[:along], *a.shape[along:]))
        at += column.shape[along]
    return tuple(done)


def sent_together(arrays, axis, dim, along):
    widths = [math.prod(a.shape[along:]) for a in arrays]
    both = jnp.concatenate(
        [a.reshape(*a.shape[:along], w) for a, w in zip(arrays, widths)], axis=along
    )
    whole = lax.psum_scatter(both, axis, scatter_dimension=dim, tiled=True)
    pieces = jnp.split(whole, [sum(widths[:k]) for k in range(1, len(widths))], axis=along)
    return tuple(
        (b.reshape(*whole.shape[:along], *a.shape[along:]) for a, b in zip(arrays, pieces))
    )


def from_everyone(shard, axis):
    size = lax.axis_size(axis)
    return lax.all_to_all(
        jnp.broadcast_to(shard[None], (size, *shard.shape)), axis, 0, 0, tiled=True
    )


def taken_together(shard, axis):
    return from_everyone(shard, axis).astype(jnp.float32).sum(axis=0)


def layer_norm(hidden, norm_gain, norm_shift):
    center = hidden - jnp.mean(hidden, axis=-1, keepdims=True)
    spread = jnp.mean(center * center, axis=-1, keepdims=True)
    return center * lax.rsqrt(spread + EPSILON) * norm_gain + norm_shift


def gelu_exact(pre_values):
    return jax.nn.gelu(pre_values, approximate=False)


def matmul(left_side, right_side):
    return jnp.dot(left_side, right_side, preferred_element_type=jnp.float32)


def matmul_left_t(left_side, right_side):
    return lax.dot_general(
        left_side, right_side, (((0,), (0,)), ((), ())), preferred_element_type=jnp.float32
    )


def matmul_right_t(left_side, right_side):
    return lax.dot_general(
        left_side, right_side, (((1,), (1,)), ((), ())), preferred_element_type=jnp.float32
    )


def head_split(row_values, seq_length):
    row_width = row_values.shape[-1]
    return row_values.reshape(-1, seq_length, row_width // HEAD_DIM, HEAD_DIM)


def masked_scores(query_heads, key_heads, valid_mask):
    scores = jnp.einsum(
        "bqhd,bkhd->bhqk", query_heads, key_heads, preferred_element_type=jnp.float32
    )
    scores = scores * HEAD_DIM ** (-0.5)
    return jnp.where(valid_mask[:, None, None, :], scores, -1000000000.0)


def split_projected(projected, seq_length):
    row_width = projected.shape[1] // 3
    return (
        head_split(projected[:, :row_width], seq_length),
        head_split(projected[:, row_width : 2 * row_width], seq_length),
        head_split(projected[:, 2 * row_width :], seq_length),
    )


def attend(projected, valid_mask):
    seq_length = valid_mask.shape[1]
    row_width = projected.shape[1] // 3
    query_heads, key_heads, value_heads = split_projected(projected, seq_length)
    scores = masked_scores(query_heads, key_heads, valid_mask)
    row_top = jnp.max(scores, axis=-1, keepdims=True)
    logsum = row_top + jnp.log(jnp.sum(jnp.exp(scores - row_top), axis=-1, keepdims=True))
    probs_low = jnp.exp(scores - logsum).astype(jnp.bfloat16)
    context = jnp.einsum(
        "bhqk,bkhd->bqhd", probs_low, value_heads, preferred_element_type=jnp.float32
    )
    return (context.reshape(-1, row_width).astype(jnp.bfloat16), logsum)


def attend_back(projected, valid_mask, logsum, grad_context):
    seq_length = valid_mask.shape[1]
    row_width = projected.shape[1] // 3
    query_heads, key_heads, value_heads = split_projected(projected, seq_length)
    scores = masked_scores(query_heads, key_heads, valid_mask)
    probs = jnp.exp(scores - logsum)
    probs_low = probs.astype(jnp.bfloat16)
    grad_heads = head_split(grad_context, seq_length)
    grad_value = jnp.einsum(
        "bhqk,bqhd->bkhd", probs_low, grad_heads, preferred_element_type=jnp.float32
    )
    grad_probs = jnp.einsum(
        "bqhd,bkhd->bhqk", grad_heads, value_heads, preferred_element_type=jnp.float32
    )
    row_inner = jnp.sum(grad_probs * probs, axis=-1, keepdims=True)
    grad_scores = (probs * (grad_probs - row_inner)).astype(jnp.bfloat16)
    scale_factor = HEAD_DIM ** (-0.5)
    grad_query = (
        jnp.einsum("bhqk,bkhd->bqhd", grad_scores, key_heads, preferred_element_type=jnp.float32)
        * scale_factor
    )
    grad_key = (
        jnp.einsum("bhqk,bqhd->bkhd", grad_scores, query_heads, preferred_element_type=jnp.float32)
        * scale_factor
    )
    return jnp.concatenate(
        [
            grad_query.reshape(-1, row_width),
            grad_key.reshape(-1, row_width),
            grad_value.reshape(-1, row_width),
        ],
        axis=1,
    ).astype(jnp.bfloat16)


def forward_pass(token_rows, attention_set, feed_set, short_mask, long_mask):
    input_weight, query_bias, value_bias, output_weight, output_bias, first_gain, first_shift = (
        attention_set
    )
    up_weight, up_bias, down_weight, down_bias, second_gain, second_shift = feed_set
    row_width = token_rows.shape[1]
    in_bias = jnp.concatenate(
        [
            query_bias.astype(jnp.float32),
            jnp.zeros((row_width,), jnp.float32),
            value_bias.astype(jnp.float32),
        ]
    )
    projected = (matmul(token_rows, input_weight) + in_bias).astype(jnp.bfloat16)
    split_row = short_mask.size
    short_context, short_logsum = attend(projected[:split_row], short_mask)
    long_context, long_logsum = attend(projected[split_row:], long_mask)
    context = jnp.concatenate([short_context, long_context], axis=0)
    first_sum = token_rows.astype(jnp.float32) + (
        matmul(context, output_weight) + output_bias.astype(jnp.float32)
    )
    first_out = layer_norm(
        first_sum, first_gain.astype(jnp.float32), first_shift.astype(jnp.float32)
    )
    first_low = first_out.astype(jnp.bfloat16)
    up_pre = matmul(first_low, up_weight) + up_bias.astype(jnp.float32)
    hidden = gelu_exact(up_pre).astype(jnp.bfloat16)
    second_sum = first_out + (matmul(hidden, down_weight) + down_bias.astype(jnp.float32))
    normed = layer_norm(
        second_sum, second_gain.astype(jnp.float32), second_shift.astype(jnp.float32)
    )
    kept = (
        projected,
        short_logsum,
        long_logsum,
        context,
        first_sum,
        first_low,
        up_pre,
        hidden,
        second_sum,
    )
    return (normed, kept)


def feed_back(grad_normed, attention_set, feed_set, kept):
    first_gain = attention_set[5]
    first_shift = attention_set[6]
    up_weight, up_bias, down_weight, down_bias, second_gain, second_shift = feed_set
    (
        projected,
        short_logsum,
        long_logsum,
        context,
        first_sum,
        first_low,
        up_pre,
        hidden,
        second_sum,
    ) = kept
    unused, second_back = jax.vjp(
        layer_norm, second_sum, second_gain.astype(jnp.float32), second_shift.astype(jnp.float32)
    )
    grad_second, grad_second_gain, grad_second_shift = second_back(grad_normed)
    grad_ffn = grad_second.astype(jnp.bfloat16)
    grad_down_weight = matmul_left_t(hidden, grad_ffn)
    grad_down_bias = jnp.sum(grad_ffn.astype(jnp.float32), axis=0)
    unused, gelu_back = jax.vjp(gelu_exact, up_pre)
    grad_up = gelu_back(matmul_right_t(grad_ffn, down_weight))[0].astype(jnp.bfloat16)
    grad_up_weight = matmul_left_t(first_low, grad_up)
    grad_up_bias = jnp.sum(grad_up.astype(jnp.float32), axis=0)
    grad_first = grad_second + matmul_right_t(grad_up, up_weight)
    unused, first_back = jax.vjp(
        layer_norm, first_sum, first_gain.astype(jnp.float32), first_shift.astype(jnp.float32)
    )
    grad_first_sum, grad_first_gain, grad_first_shift = first_back(grad_first)
    feed_grads = (
        grad_up_weight,
        grad_up_bias,
        grad_down_weight,
        grad_down_bias,
        grad_second_gain,
        grad_second_shift,
        grad_first_gain,
        grad_first_shift,
    )
    return (grad_first_sum, feed_grads)


def attention_back(token_rows, grad_first_sum, attention_set, kept, short_mask, long_mask):
    input_weight = attention_set[0]
    output_weight = attention_set[3]
    (
        projected,
        short_logsum,
        long_logsum,
        context,
        first_sum,
        first_low,
        up_pre,
        hidden,
        second_sum,
    ) = kept
    row_width = token_rows.shape[1]
    grad_attended = grad_first_sum.astype(jnp.bfloat16)
    grad_output_weight = matmul_left_t(context, grad_attended)
    grad_output_bias = jnp.sum(grad_attended.astype(jnp.float32), axis=0)
    grad_context = matmul_right_t(grad_attended, output_weight).astype(jnp.bfloat16)
    split_row = short_mask.size
    grad_projected = jnp.concatenate(
        [
            attend_back(projected[:split_row], short_mask, short_logsum, grad_context[:split_row]),
            attend_back(projected[split_row:], long_mask, long_logsum, grad_context[split_row:]),
        ],
        axis=0,
    )
    grad_input_weight = matmul_left_t(token_rows, grad_projected)
    bias_sums = jnp.sum(grad_projected.astype(jnp.float32), axis=0)
    grad_query_bias = bias_sums[:row_width]
    grad_value_bias = bias_sums[2 * row_width :]
    grad_rows = grad_first_sum + matmul_right_t(grad_projected, input_weight)
    attention_grads = (
        grad_input_weight,
        grad_query_bias,
        grad_value_bias,
        grad_output_weight,
        grad_output_bias,
    )
    return (grad_rows, attention_grads)


def on_device(
    short_tokens,
    long_tokens,
    short_lengths,
    long_lengths,
    short_cotangent,
    long_cotangent,
    input_weight,
    query_bias,
    value_bias,
    output_weight,
    output_bias,
    first_gain,
    first_shift,
    up_weight,
    up_bias,
    down_weight,
    down_bias,
    second_gain,
    second_shift,
):
    short_count, short_length, row_width = short_tokens.shape
    long_count, long_length, unused_width = long_tokens.shape
    short_mask = (
        lax.broadcasted_iota(jnp.int32, (short_count, short_length), 1) < short_lengths[:, None]
    )
    long_mask = (
        lax.broadcasted_iota(jnp.int32, (long_count, long_length), 1) < long_lengths[:, None]
    )
    token_rows = jnp.concatenate(
        [short_tokens.reshape(-1, row_width), long_tokens.reshape(-1, row_width)], axis=0
    )
    cot_rows = jnp.concatenate(
        [short_cotangent.reshape(-1, row_width), long_cotangent.reshape(-1, row_width)], axis=0
    )
    valid_rows = jnp.concatenate([short_mask.reshape(-1), long_mask.reshape(-1)]).astype(
        jnp.float32
    )
    split_row = short_mask.size

    def fetch_attention():
        return in_one_piece(
            (
                input_weight,
                query_bias,
                value_bias,
                output_weight,
                output_bias,
                first_gain,
                first_shift,
            ),
            "shard",
            0,
            1,
        )

    def fetch_feed():
        return (
            lax.all_gather(up_weight, "shard", axis=0, tiled=True),
            *in_one_piece((up_bias, down_weight), "shard", 0, 1),
            lax.all_gather(down_bias, "shard", axis=0, tiled=True),
            lax.all_gather(second_gain, "shard", axis=0, tiled=True),
            lax.all_gather(second_shift, "shard", axis=0, tiled=True),
        )

    attention_set = fetch_attention()
    feed_set = fetch_feed()
    normed, kept = forward_pass(token_rows, attention_set, feed_set, short_mask, long_mask)
    out_rows = (normed * valid_rows[:, None]).astype(jnp.bfloat16)
    attention_set = fetch_attention()
    feed_set = fetch_feed()
    unused_normed, kept = forward_pass(token_rows, attention_set, feed_set, short_mask, long_mask)
    grad_normed = cot_rows.astype(jnp.float32) * valid_rows[:, None]
    grad_first_sum, feed_grads = feed_back(grad_normed, attention_set, feed_set, kept)
    feed_parts = (
        lax.psum_scatter(
            feed_grads[0].astype(jnp.bfloat16), "shard", scatter_dimension=0, tiled=True
        ).astype(jnp.float32),
        *tuple(
            (
                part.astype(jnp.float32)
                for part in sent_together(
                    (feed_grads[1].astype(jnp.bfloat16), feed_grads[2].astype(jnp.bfloat16)),
                    "shard",
                    0,
                    1,
                )
            )
        ),
        lax.psum_scatter(
            feed_grads[3].astype(jnp.bfloat16), "shard", scatter_dimension=0, tiled=True
        ).astype(jnp.float32),
        lax.psum_scatter(
            feed_grads[4].astype(jnp.bfloat16), "shard", scatter_dimension=0, tiled=True
        ).astype(jnp.float32),
        lax.psum_scatter(
            feed_grads[5].astype(jnp.bfloat16), "shard", scatter_dimension=0, tiled=True
        ).astype(jnp.float32),
        lax.psum_scatter(
            feed_grads[6].astype(jnp.bfloat16), "shard", scatter_dimension=0, tiled=True
        ).astype(jnp.float32),
        lax.psum_scatter(
            feed_grads[7].astype(jnp.bfloat16), "shard", scatter_dimension=0, tiled=True
        ).astype(jnp.float32),
    )
    feed_owned = (
        taken_together(feed_parts[0].astype(jnp.bfloat16), "rep").astype(jnp.float32),
        taken_together(feed_parts[1].astype(jnp.bfloat16), "rep").astype(jnp.float32),
        taken_together(feed_parts[2].astype(jnp.bfloat16), "rep").astype(jnp.float32),
        taken_together(feed_parts[3].astype(jnp.bfloat16), "rep").astype(jnp.float32),
        taken_together(feed_parts[4].astype(jnp.bfloat16), "rep").astype(jnp.float32),
        taken_together(feed_parts[5].astype(jnp.bfloat16), "rep").astype(jnp.float32),
        taken_together(feed_parts[6].astype(jnp.bfloat16), "rep").astype(jnp.float32),
        taken_together(feed_parts[7].astype(jnp.bfloat16), "rep").astype(jnp.float32),
    )
    grad_rows, attention_grads = attention_back(
        token_rows, grad_first_sum, attention_set, kept, short_mask, long_mask
    )
    attention_parts = tuple(
        (
            part.astype(jnp.float32)
            for part in sent_together(
                (
                    attention_grads[0].astype(jnp.bfloat16),
                    attention_grads[1].astype(jnp.bfloat16),
                    attention_grads[2].astype(jnp.bfloat16),
                    attention_grads[3].astype(jnp.bfloat16),
                    attention_grads[4].astype(jnp.bfloat16),
                ),
                "shard",
                0,
                1,
            )
        )
    )
    attention_owned = (
        taken_together(attention_parts[0].astype(jnp.bfloat16), "rep").astype(jnp.float32),
        taken_together(attention_parts[1].astype(jnp.bfloat16), "rep").astype(jnp.float32),
        taken_together(attention_parts[2].astype(jnp.bfloat16), "rep").astype(jnp.float32),
        taken_together(attention_parts[3].astype(jnp.bfloat16), "rep").astype(jnp.float32),
        taken_together(attention_parts[4].astype(jnp.bfloat16), "rep").astype(jnp.float32),
    )
    short_out = out_rows[:split_row].reshape(short_tokens.shape)
    long_out = out_rows[split_row:].reshape(long_tokens.shape)
    short_grad = grad_rows[:split_row].reshape(short_tokens.shape)
    long_grad = grad_rows[split_row:].reshape(long_tokens.shape)
    return (
        short_out,
        long_out,
        short_grad,
        long_grad,
        attention_owned[0],
        attention_owned[1],
        attention_owned[2],
        attention_owned[3],
        attention_owned[4],
        feed_owned[6],
        feed_owned[7],
        feed_owned[0],
        feed_owned[1],
        feed_owned[2],
        feed_owned[3],
        feed_owned[4],
        feed_owned[5],
    )


def solution(mesh):
    return jax.shard_map(
        on_device,
        mesh=mesh,
        in_specs=(
            P(("rep", "shard"), None, None),
            P(("rep", "shard"), None, None),
            P(("rep", "shard")),
            P(("rep", "shard")),
            P(("rep", "shard"), None, None),
            P(("rep", "shard"), None, None),
            P("shard", None),
            P("shard"),
            P("shard"),
            P("shard", None),
            P("shard"),
            P("shard"),
            P("shard"),
            P("shard", None),
            P("shard"),
            P("shard", None),
            P("shard"),
            P("shard"),
            P("shard"),
        ),
        out_specs=(
            P(("rep", "shard"), None, None),
            P(("rep", "shard"), None, None),
            P(("rep", "shard"), None, None),
            P(("rep", "shard"), None, None),
            P("shard", None),
            P("shard"),
            P("shard"),
            P("shard", None),
            P("shard"),
            P("shard"),
            P("shard"),
            P("shard", None),
            P("shard"),
            P("shard", None),
            P("shard"),
            P("shard"),
            P("shard"),
        ),
        check_vma=False,
    )
```

profile of v0, /device:TPU:0, one launch (start us, length us, event | category | flops | bytes accessed | tf_op | source)
XLA Modules:
  0.0 606.5 jit_solution(9714779446159635348)
XLA Ops:
  8.0 1.7 pad_maximum_fusion.10
  13.5 1.7 concatenate.47
  19.7 68.8 %all-reduce.10 = (bf16[768]{0:T(1024)(128)(2,1)S(1)}, bf16[768]{0:T(1024)(128)(2,1)S(1)}) all-reduce(bf16[768]{0:T(1024)(128)(2,1)S(1)} %dynamic-update-slice, bf16[768]{0:T(1024)(128)(2,1)S(1)} %dynamic-update-slice.1), channel_id=1, replica_groups=mesh['rep'=4,'shard'=32] {'shard'}, use_global_device_ids=true, to_apply=%add | all-reduce | flops 1536 | bytes 6144
  91.5 19.2 %all-gather.4.cloned.1.call-done = bf16[768,3077]{1,0:T(8,128)(2,1)} async-done(((bf16[24,3077]{1,0:T(8,128)(2,1)}), bf16[768,3077]{1,0:T(8,128)(2,1)}) %all-gather.4.cloned.1.call-update) | async-done | bytes 4726288 | tf_op jit(solution)/shard_map/all_gather | solution.py:17
  110.7 1.9 convert_reduce_fusion.5
  112.7 4.8 add_convert_fusion.1
  122.4 2.9 fusion.72
  127.9 2.3 copy.306
  130.1 2.2 reshape.440
  133.5 2.2 reshape.439
  135.8 1.8 fusion.6
  141.9 3.0 fusion.77
  145.3 13.9 %all-gather.6.cloned.1.call-done = bf16[768,3072]{1,0:T(8,128)(2,1)} async-done(((bf16[24,3072]{1,0:T(8,128)(2,1)}), bf16[768,3072]{1,0:T(8,128)(2,1)}) %all-gather.6.cloned.1.call-update) | async-done | bytes 4718608 | tf_op jit(solution)/shard_map/all_gather | solution.py:334
  159.2 24.0 %multiply_convert_fusion = (bf16[640,3072]{1,0:T(8,128)(2,1)S(1)}, f32[640,3072]{1,0:T(8,128)}, f32[640,3072]{1,0:T(8,128)}) fusion(f32[3072]{0:T(1024)S(1)} %convert_reduce_fusion, bf16[768,3072]{1,0:T(8,128)(2,1)} %all-gather.6.cloned.1.call-done, f32[640,768]{1,0:T(8,128)S(1)} %get-tuple-element.64, f32[768]{0:T(1024)S(1)} %get-tuple-element.21, ...), kind=kOutput, calls=%fused_computation.3 | convolution fusion | flops 3152117760 | bytes 26369024 | tf_op jit(solution)/shard_map/dot_general | solution.py:59
  183.3 7.8 %fusion.78 = (f32[640]{0:T(1024)S(1)}, f32[640,768]{1,0:T(8,128)S(1)}) fusion(f32[768]{0:T(1024)S(1)} %convert_element_type.282, bf16[640,3072]{1,0:T(8,128)(2,1)S(1)} %get-tuple-element.47, bf16[3072,769]{1,0:T(8,128)(2,1)} %all-gather.8.cloned.1.call-done, f32[768]{0:T(1024)S(1)} %get-tuple-element.21, f32[768]{0:T(1024)S(1)} %get-tuple-element.20, ...), kind=kOutput, calls=%fused_computation.167 | convolution fusion | flops 3023339008 | bytes 12599808 | tf_op jit(solution)/shard_map/dot_general | solution.py:59
  194.8 11.0 %fusion.79 = (bf16[3072]{0:T(1024)(128)(2,1)}, bf16[640,3072]{1,0:T(8,128)(2,1)S(1)}) fusion(f32[640,3072]{1,0:T(8,128)} %get-tuple-element.48, bf16[640,768]{1,0:T(8,128)(2,1)S(1)} %get-tuple-element.44, bf16[3072,769]{1,0:T(8,128)(2,1)S(1)} %bitcast.111, f32[640,3072]{1,0:T(8,128)} %get-tuple-element.65, f32[3072]{0:T(1024)S(1)} %convert_reduce_fusion), kind=kOutput, calls=%fused_computation.168 | convolution fusion | flops 3051353088 | bytes 25380864 | tf_op jit(solution)/shard_map/dot_general | solution.py:69
  205.8 4.3 multiply_reduce_fusion.2
  210.1 2.0 fusion.68
  212.1 2.4 fusion.67
  215.4 2.4 convolution_convert_fusion.4
  219.9 3.1 reshape.450
  223.0 5.8 multiply_reduce_fusion
  228.9 2.1 multiply_convert_fusion.1
  232.5 2.0 fusion.25
  234.5 2.5 fusion.28
  242.7 2.1 convolution_convert_fusion.3
  258.4 1.8 constant_dynamic-update-slice_fusion.3
  260.2 1.6 constant_dynamic-update-slice_fusion.2
  261.8 5.8 convolution_convert_fusion.2
  267.7 2.0 reduce.13
  274.6 8.6 %concatenate.56 = bf16[768,3075]{1,0:T(8,128)(2,1)} concatenate(bf16[768,2304]{1,0:T(8,128)(2,1)} %convolution_convert_fusion.2, bf16[768,1]{1,0:T(8,128)(2,1)} %reshape.481, bf16[768,1]{1,0:T(8,128)(2,1)} %reshape.482, bf16[768,768]{1,0:T(8,128)(2,1)S(1)} %copy-done.19, bf16[768,1]{1,0:T(8,128)(2,1)} %reshape.483), dimensions={1} | concatenate | bytes 9446400 | tf_op jit(solution)/shard_map/concatenate | solution.py:27
  284.4 6.2 %convolution_convert_fusion = bf16[3072,768]{0,1:T(8,128)(2,1)S(1)} fusion(bf16[640,3072]{1,0:T(8,128)(2,1)} %copy-done.51, bf16[640,768]{1,0:T(8,128)(2,1)S(1)} %copy-done.23), kind=kOutput, calls=%fused_computation.23 | convolution fusion | flops 3022258176 | bytes 9633792 | tf_op jit(solution)/shard_map/dot_general | solution.py:63
  290.6 3.4 pad_maximum_fusion
  294.0 7.5 %copy.364 = bf16[3072,769]{1,0:T(8,128)(2,1)} copy(bf16[3072,769]{0,1:T(8,128)(2,1)} %pad_maximum_fusion) | data formatting | bytes 9449472
  303.1 8.0 %convolution_convert_fusion.1 = bf16[768,3072]{1,0:T(8,128)(2,1)} fusion(bf16[640,3072]{1,0:T(8,128)(2,1)} %copy-done.52, f32[640,768]{1,0:T(8,128)S(1)} %copy-done.4, f32[768]{0:T(1024)S(1)} %copy-done.43, f32[768]{0:T(1024)S(1)} %copy-done.33, f32[640]{0:T(1024)S(1)} %copy-done.35, f32[640]{0:T(1024)S(1)} %copy-done.31), kind=kOutput, calls=%fused_computation.24 | convolution fusion | flops 3024715776 | bytes 10628096 | tf_op jit(solution)/shard_map/dot_general | solution.py:63
  312.7 126.8 %all-reduce.9 = (bf16[768]{0:T(1024)(128)(2,1)S(1)}, bf16[768]{0:T(1024)(128)(2,1)S(1)}, bf16[768]{0:T(1024)(128)(2,1)S(1)}, bf16[768]{0:T(1024)(128)(2,1)S(1)},...) all-reduce(bf16[768]{0:T(1024)(128)(2,1)S(1)} %dynamic-update-slice, ...), channel_id=1, replica_groups=mesh['rep'=4,'shard'=32] {'shard'}, use_global_device_ids=true, to_apply=%add.2 | all-reduce | flops 4608 | bytes 18432
  440.1 4.3 all-to-all-start.5
  444.4 7.8 %add_add_fusion.4 = f32[640,768]{1,0:T(8,128)} fusion(f32[640,768]{1,0:T(8,128)} %get-tuple-element.42, bf16[768,3077]{1,0:T(8,128)(2,1)} %all-gather.4.cloned.1.call-done, bf16[512,2304]{0,1:T(8,128)(2,1)} %copy-done.9, bf16[128,2304]{0,1:T(8,128)(2,1)S(1)} %copy-done.20, f32[640]{0:T(1024)S(1)} %copy-done.37), kind=kOutput, calls=%fused_computation.52 | convolution fusion | flops 2271805440 | bytes 10422784 | tf_op jit(solution)/shard_map/dot_general | solution.py:69
  452.8 4.8 all-to-all-start.6
  457.7 5.1 all-to-all-done.6
  463.4 3.2 all-to-all-start.10
  466.7 5.1 all-to-all-done.10
  472.4 3.2 all-to-all-start.11
  475.7 5.1 all-to-all-done.11
  481.3 3.2 all-to-all-start.12
  485.6 4.1 all-to-all-done.12
  490.3 3.2 all-to-all-start.1
  494.7 4.0 all-to-all-done.1
  499.2 3.2 all-to-all-start.2
  503.4 1.8 slice.146
  505.2 2.4 all-to-all-done.2
  508.2 3.2 all-to-all-start.4
  511.4 2.7 slice.147
  517.3 3.3 all-to-all-start.3
  521.5 5.1 all-to-all-done.3
  527.4 3.5 all-to-all-start
  533.3 5.2 all-to-all-done
  539.1 3.2 all-to-all-start.8
  542.9 28.2 %reduce-scatter.5.cloned.1.call-done = bf16[24,3072]{1,0:T(8,128)(2,1)} async-done(((bf16[768,3072]{1,0:T(8,128)(2,1)}), bf16[24,3072]{1,0:T(8,128)(2,1)}) %reduce-scatter.5.cloned.1.call-update) | async-done | bytes 147472 | tf_op jit(solution)/shard_map/reduce_scatter | solution.py:351
  571.1 1.8 broadcast_in_dim.100
  572.9 4.3 all-to-all-start.7
  580.3 5.4 all-to-all-done.7
  586.5 3.5 all-to-all-start.9
  592.7 5.7 all-to-all-done.9
  (272 shorter events, 84.3 us)
Async XLA Ops:
  7.2 82.9 %all-gather.8.cloned.1.call-start = ((), (), s32[]{:S(2)}) async-start(), calls=%async_computation.17 | async-start | bytes 5677056 | tf_op jit(solution)/shard_map/all_gather | solution.py:17
  9.7 100.9 %all-gather.4.cloned.1.call-start = ((), (), s32[]{:S(2)}) async-start(), calls=%async_computation.15 | async-start | bytes 5068800 | tf_op jit(solution)/shard_map/all_gather | solution.py:17
  15.2 144.0 %all-gather.6.cloned.1.call-start = ((), (), s32[]{:S(2)}) async-start(), calls=%async_computation.16 | async-start | bytes 4866048 | tf_op jit(solution)/shard_map/all_gather | solution.py:334
  15.9 468.6 %all-reduce.13.cloned.1.call-start = ((), (), s32[]{:S(2)}) async-start(), calls=%async_computation.20 | async-start | bytes 9830400
  112.6 70.6 %copy-start.42 = (f32[768]{0:T(1024)}, f32[768]{0:T(1024)S(1)}, u32[]{:S(2)}) copy-start(f32[768]{0:T(1024)S(1)} %get-tuple-element.21) | copy-start | bytes 9220
  112.6 97.5 %copy-start.32 = (f32[768]{0:T(1024)}, f32[768]{0:T(1024)S(1)}, u32[]{:S(2)}) copy-start(f32[768]{0:T(1024)S(1)} %get-tuple-element.20) | copy-start | bytes 9220
  117.5 1.6 copy-start.18
  119.4 2.8 copy-start.12
  120.9 4.4 copy-start.10
  132.4 5.2 copy-start.5
  135.8 1.8 copy-start.7
  137.6 3.2 copy-start
  137.6 1.7 copy-start.16
  141.9 3.4 copy-start.28
  144.9 65.2 %copy-start.3 = (f32[640,768]{1,0:T(8,128)}, f32[640,768]{1,0:T(8,128)S(1)}, u32[]{:S(2)}) copy-start(f32[640,768]{1,0:T(8,128)S(1)} %get-tuple-element.64) | copy-start | bytes 5898244
  144.9 65.2 %copy-start.30 = (f32[640]{0:T(1024)}, f32[640]{0:T(1024)S(1)}, u32[]{:S(2)}) copy-start(f32[640]{0:T(1024)S(1)} %broadcast_multiply_fusion.1) | copy-start | bytes 7684
  145.3 64.8 %copy-start.34 = (f32[640]{0:T(1024)}, f32[640]{0:T(1024)S(1)}, u32[]{:S(2)}) copy-start(f32[640]{0:T(1024)S(1)} %fusion.55) | copy-start | bytes 7684
  183.2 7.9 %copy-start.51 = (bf16[640,3072]{1,0:T(8,128)(2,1)}, bf16[640,3072]{1,0:T(8,128)(2,1)S(1)}, u32[]{:S(2)}) copy-start(bf16[640,3072]{1,0:T(8,128)(2,1)S(1)} %get-tuple-element.47) | copy-start | bytes 11796484
  183.3 8.3 %copy-start.15 = (bf16[2,256,768]{2,1,0:T(8,128)(2,1)S(1)}, bf16[2,256,768]{2,1,0:T(8,128)(2,1)}, u32[]{:S(2)}) copy-start(bf16[2,256,768]{2,1,0:T(8,128)(2,1)} %param.24) | copy-start | bytes 2359300
  183.3 8.3 %copy-start.26 = (bf16[2,64,768]{2,1,0:T(8,128)(2,1)S(1)}, bf16[2,64,768]{2,1,0:T(8,128)(2,1)}, u32[]{:S(2)}) copy-start(bf16[2,64,768]{2,1,0:T(8,128)(2,1)} %param.23) | copy-start | bytes 589828
  191.1 2.8 copy-start.1
  191.1 3.6 slice-start.3
  193.0 1.7 slice-start.4
  193.0 12.7 %slice-start.5 = ((s8[4718592]{0:T(1024)(128)(4,1)}), s8[4194304]{0:T(1024)(128)(4,1)S(1)}, s32[]{:S(2)}) async-start(s8[4718592]{0:T(1024)(128)(4,1)} %bitcast.119), calls=%async_computation.26 | async-start | bytes 8388608
  194.8 11.0 %copy-start.22 = (bf16[640,768]{1,0:T(8,128)(2,1)}, bf16[640,768]{1,0:T(8,128)(2,1)S(1)}, u32[]{:S(2)}) copy-start(bf16[640,768]{1,0:T(8,128)(2,1)S(1)} %get-tuple-element.44) | copy-start | bytes 2949124
  194.8 11.0 %slice-start.6 = ((s8[4718592]{0:T(1024)(128)(4,1)}), s8[524288]{0:T(1024)(128)(4,1)S(1)}, s32[]{:S(2)}) async-start(s8[4718592]{0:T(1024)(128)(4,1)} %bitcast.119), calls=%async_computation.27 | async-start | bytes 1048576
  205.7 4.3 copy-start.52
  212.1 5.8 copy-start.36
  219.9 8.9 %slice-start = ((s8[6291456]{0:T(1024)(128)(4,1)}), s8[2097152]{0:T(1024)(128)(4,1)S(1)}, s32[]{:S(2)}) async-start(s8[6291456]{0:T(1024)(128)(4,1)} %bitcast.92), calls=%async_computation.21 | async-start | bytes 4194304
  223.0 5.8 slice-start.1
  228.8 2.2 copy-start.6
  231.0 3.4 copy-start.17
  234.5 2.5 slice-start.2
  236.9 2.5 copy-start.11
  237.7 5.1 copy-start.25
  237.7 5.1 copy-start.29
  242.7 2.1 copy-start.14
  244.8 2.1 copy-start.27
  257.0 4.8 copy-start.47
  257.0 4.8 copy-start.49
  258.3 24.8 %copy-start.9 = (bf16[512,2304]{0,1:T(8,128)(2,1)}, bf16[512,2304]{0,1:T(8,128)(2,1)S(1)}, u32[]{:S(2)}) copy-start(bf16[512,2304]{0,1:T(8,128)(2,1)S(1)} %constant_dynamic-update-slice_fusion.5) | copy-start | bytes 7077892
  267.7 6.9 %copy-start.19 = (bf16[768,768]{1,0:T(8,128)(2,1)S(1)}, bf16[768,768]{1,0:T(8,128)(2,1)}, u32[]{:S(2)}) copy-start(bf16[768,768]{1,0:T(8,128)(2,1)} %convolution_convert_fusion.3) | copy-start | bytes 3538948
  283.2 249.3 %reduce-scatter.7.cloned.1.call-start = ((), (), s32[]{:S(2)}) async-start(), calls=%async_computation.19 | async-start | bytes 5677056
  301.5 1.5 copy-start.4
  301.5 1.5 copy-start.31
  301.5 1.5 copy-start.33
  301.5 1.5 copy-start.35
  301.6 269.5 %reduce-scatter.5.cloned.1.call-start = ((), (), s32[]{:S(2)}) async-start(), calls=%async_computation.18 | async-start | bytes 4866048 | tf_op jit(solution)/shard_map/reduce_scatter | solution.py:351
  311.2 133.2 %copy-start.20 = (bf16[128,2304]{0,1:T(8,128)(2,1)S(1)}, bf16[128,2304]{0,1:T(8,128)(2,1)}, u32[]{:S(2)}) copy-start(bf16[128,2304]{0,1:T(8,128)(2,1)} %constant_dynamic-update-slice_fusion.2) | copy-start | bytes 1769476
  311.2 133.2 %copy-start.37 = (f32[640]{0:T(1024)S(1)}, f32[640]{0:T(1024)}, u32[]{:S(2)}) copy-start(f32[640]{0:T(1024)} %copy-done.36) | copy-start | bytes 7684
  440.1 12.2 %all-to-all-start.5 = ((bf16[4,1,24]{2,1,0:T(2,128)(2,1)}), bf16[4,1,24]{2,1,0:T(2,128)(2,1)S(1)}, u32[]{:S(2)}, u32[]{:S(2)}) async-start(bf16[4,1,24]{2,1,0:T(2,128)(2,1)} %broadcast_in_dim.98), calls=%async_computation.5 | async-start | bytes 4096 | tf_op jit(solution)/shard_map/all_to_all | solution.py:39
  444.4 49.2 %copy-start.2 = (f32[640,768]{1,0:T(8,128)S(1)}, f32[640,768]{1,0:T(8,128)}, u32[]{:S(2)}) copy-start(f32[640,768]{1,0:T(8,128)} %copy-done.1) | copy-start | bytes 5898244
  452.8 10.0 %all-to-all-start.6 = ((bf16[4,1,24]{2,1,0:T(2,128)(2,1)}), bf16[4,1,24]{2,1,0:T(2,128)(2,1)S(1)}, u32[]{:S(2)}, u32[]{:S(2)}) async-start(bf16[4,1,24]{2,1,0:T(2,128)(2,1)} %broadcast_in_dim.99), calls=%async_computation.6 | async-start | bytes 4096 | tf_op jit(solution)/shard_map/all_to_all | solution.py:39
  463.4 8.4 %all-to-all-start.10 = ((bf16[4,1,24]{2,1,0:T(2,128)(2,1)}), bf16[4,1,24]{2,1,0:T(2,128)(2,1)S(1)}, u32[]{:S(2)}, u32[]{:S(2)}) async-start(bf16[4,1,24]{2,1,0:T(2,128)(2,1)} %broadcast_in_dim.104), calls=%async_computation.11 | async-start | bytes 4096 | tf_op jit(solution)/shard_map/all_to_all | solution.py:39
  472.4 8.4 %all-to-all-start.11 = ((bf16[4,1,24]{2,1,0:T(2,128)(2,1)}), bf16[4,1,24]{2,1,0:T(2,128)(2,1)S(1)}, u32[]{:S(2)}, u32[]{:S(2)}) async-start(bf16[4,1,24]{2,1,0:T(2,128)(2,1)} %broadcast_in_dim.105), calls=%async_computation.12 | async-start | bytes 4096 | tf_op jit(solution)/shard_map/all_to_all | solution.py:39
  481.3 8.4 %all-to-all-start.12 = ((bf16[4,1,24]{2,1,0:T(2,128)(2,1)}), bf16[4,1,24]{2,1,0:T(2,128)(2,1)S(1)}, u32[]{:S(2)}, u32[]{:S(2)}) async-start(bf16[4,1,24]{2,1,0:T(2,128)(2,1)} %broadcast_in_dim.106), calls=%async_computation.13 | async-start | bytes 4096 | tf_op jit(solution)/shard_map/all_to_all | solution.py:39
  490.3 8.4 %all-to-all-start.1 = ((bf16[4,1,24]{2,1,0:T(2,128)(2,1)}), bf16[4,1,24]{2,1,0:T(2,128)(2,1)S(1)}, u32[]{:S(2)}, u32[]{:S(2)}) async-start(bf16[4,1,24]{2,1,0:T(2,128)(2,1)} %broadcast_in_dim.92), calls=%async_computation.1 | async-start | bytes 4096 | tf_op jit(solution)/shard_map/all_to_all | solution.py:39
  499.2 8.4 %all-to-all-start.2 = ((bf16[4,1,24]{2,1,0:T(2,128)(2,1)}), bf16[4,1,24]{2,1,0:T(2,128)(2,1)S(1)}, u32[]{:S(2)}, u32[]{:S(2)}) async-start(bf16[4,1,24]{2,1,0:T(2,128)(2,1)} %broadcast_in_dim.94), calls=%async_computation.2 | async-start | bytes 4096 | tf_op jit(solution)/shard_map/all_to_all | solution.py:39
  508.2 8.4 %all-to-all-start.4 = ((bf16[4,1,24]{2,1,0:T(2,128)(2,1)}), bf16[4,1,24]{2,1,0:T(2,128)(2,1)S(1)}, u32[]{:S(2)}, u32[]{:S(2)}) async-start(bf16[4,1,24]{2,1,0:T(2,128)(2,1)} %broadcast_in_dim.97), calls=%async_computation.4 | async-start | bytes 4096 | tf_op jit(solution)/shard_map/all_to_all | solution.py:39
  517.3 9.4 %all-to-all-start.3 = ((bf16[4,24,768]{2,1,0:T(8,128)(2,1)}), bf16[4,24,768]{2,1,0:T(8,128)(2,1)S(1)}, u32[]{:S(2)}, u32[]{:S(2)}) async-start(bf16[4,24,768]{2,1,0:T(8,128)(2,1)} %broadcast_in_dim.95), calls=%async_computation.3 | async-start | bytes 294912 | tf_op jit(solution)/shard_map/all_to_all | solution.py:39
  527.4 11.1 %all-to-all-start = ((bf16[4,24,2304]{2,1,0:T(8,128)(2,1)}), bf16[4,24,2304]{2,1,0:T(8,128)(2,1)S(1)}, u32[]{:S(2)}, u32[]{:S(2)}) async-start(bf16[4,24,2304]{2,1,0:T(8,128)(2,1)} %broadcast_in_dim.90), calls=%async_computation | async-start | bytes 884736 | tf_op jit(solution)/shard_map/all_to_all | solution.py:39
  539.1 32.0 %all-to-all-start.8 = ((bf16[4,1,96]{2,1,0:T(2,128)(2,1)}), bf16[4,1,96]{2,1,0:T(2,128)(2,1)S(1)}, u32[]{:S(2)}, u32[]{:S(2)}) async-start(bf16[4,1,96]{2,1,0:T(2,128)(2,1)} %broadcast_in_dim.102), calls=%async_computation.9 | async-start | bytes 4096 | tf_op jit(solution)/shard_map/all_to_all | solution.py:39
  572.9 12.8 %all-to-all-start.7 = ((bf16[4,24,3072]{2,1,0:T(8,128)(2,1)}), bf16[4,24,3072]{2,1,0:T(8,128)(2,1)S(1)}, u32[]{:S(2)}, u32[]{:S(2)}) async-start(bf16[4,24,3072]{2,1,0:T(8,128)(2,1)} %broadcast_in_dim.100), calls=%async_computation.8 | async-start | bytes 1179648 | tf_op jit(solution)/shard_map/all_to_all | solution.py:39
  586.5 11.9 %all-to-all-start.9 = ((bf16[4,96,768]{2,1,0:T(8,128)(2,1)}), bf16[4,96,768]{2,1,0:T(8,128)(2,1)S(1)}, u32[]{:S(2)}, u32[]{:S(2)}) async-start(bf16[4,96,768]{2,1,0:T(8,128)(2,1)} %broadcast_in_dim.103), calls=%async_computation.10 | async-start | bytes 1179648 | tf_op jit(solution)/shard_map/all_to_all | solution.py:39
  (15 other events, 18.4 us)
Sparse Core Ops, SparseCore 0:
  10.8 50.4 all-gather.7
  64.2 46.4 all-gather.3
  112.9 46.2 all-gather.5
  283.3 112.7 all-reduce.12
  399.7 84.6 reduce-scatter.6
  488.0 82.9 reduce-scatter.4
where the time goes:
time: 617 us; the launch traced here: 606 us
  blocking collectives  196 us (32%)
  waiting for transfers between devices  111 us (18%)
  matrix products  108 us (18%)
  local copies, waits for them, and re-layouts  95 us (15%)
  starting transfers between devices  46.5 us (8%)
  other arithmetic  34 us (6%)
  between operations  17 us (3%)
    unnamed x2, blocking collectives  196 us
    all_to_all x13, waiting for transfers between devices, from_everyone(): lax.all_to_all(jnp.broadcast_to(shard[None], (size, *shard.shape)), axis,...  48.7 us
    all_to_all x13, starting transfers between devices, from_everyone(): lax.all_to_all(jnp.broadcast_to(shard[None], (size, *shard.shape)), axis,...  46.2 us
    dot_general x4, matrix products, matmul(): return jnp.dot(left_side, right_side, preferred_element_type=jnp.float32)  39.6 us
    reduce_scatter x1, waiting for transfers between devices, on_device(): lax.psum_scatter(feed_grads[0].astype(jnp.bfloat16), 'shard', scatter_dim...  28.2 us
    dot_general x4, matrix products, matmul_right_t(): lax.dot_general(left_side, right_side, (((1,), (1,)), ((), ())), preferre...  25.5 us
    unnamed x141, local copies, waits for them, and re-layouts  23.4 us
    dot_general x4, matrix products, matmul_left_t(): lax.dot_general(left_side, right_side, (((0,), (0,)), ((), ())), preferre...  22.2 us
  transfers between devices with their start and end apart: 19, of which 14 were waited for; matrix products, arithmetic and copies ran while one was open for 17% of the time, Pallas kernels for 0%

commit v1 on v0

v1 whole, which is shorter than its diff:
```python
import functools

import jax
import jax.numpy as jnp
from jax import lax
from jax.experimental import pallas as pl
from jax.experimental.pallas import tpu as pltpu
from jax.sharding import PartitionSpec as P

F32 = jnp.float32
BF16 = jnp.bfloat16
HEAD_DIM = 64
PAIR = 128
EPSILON = 1e-06
QB, VB, OB, G1, S1, DB, G2, S2 = range(8)
VMEM_LIMIT = 56 * 1024 * 1024
RING = 4
CHIPS = RING * RING
SHARDS = 2 * CHIPS


def nn(a, b):
    return lax.dot_general(a, b, (((1,), (0,)), ((), ())), preferred_element_type=F32)


def nt(a, b):
    return lax.dot_general(a, b, (((1,), (1,)), ((), ())), preferred_element_type=F32)


def tn(a, b):
    return lax.dot_general(a, b, (((0,), (0,)), ((), ())), preferred_element_type=F32)


def iota(shape, dim):
    return lax.broadcasted_iota(jnp.int32, shape, dim)


def row_of(ref, i):
    return ref[i : i + 1, :].astype(F32)


def whole(*shape):
    return pl.BlockSpec(shape, lambda g, *_: (0,) * len(shape))


def params():
    return pltpu.CompilerParams(vmem_limit_bytes=VMEM_LIMIT)


def cost(flops, moved):
    return pl.CostEstimate(flops=int(flops), bytes_accessed=int(moved), transcendentals=0)


def places(pos, x, z):
    along_x, along_z = (x - pos[0]) & (RING - 1), (z - pos[1]) & (RING - 1)
    return along_x * RING + along_z, along_z * RING + along_x


def deal(keep, give, pos, value, at, each):
    first = pos[2] == 0
    for x in range(RING):
        for z in range(RING):
            p0, p1 = places(pos, x, z)
            low = 2 * (x * RING + z) * each
            even, odd = value[low : low + each], value[low + each : low + 2 * each]
            keep[jnp.where(first, p0, p1), at] = jnp.where(first, even, odd)
            give[jnp.where(first, p1, p0), at] = jnp.where(first, odd, even)


def spread(owners, width):
    each = width // owners
    at = iota((owners, width), 1)
    low = iota((owners, width), 0) * each
    return (at >= low) & (at < low + each)


def column_rest(rows, width, each):
    at = iota((rows, width), 1)
    return at - (at // each) * each


def two_heads(pair):
    low_half = iota(pair.shape, 1) < HEAD_DIM
    zero = jnp.zeros_like(pair)
    return jnp.concatenate([jnp.where(low_half, pair, zero), jnp.where(low_half, zero, pair)], axis=0)


def own_lanes(stack):
    half = stack.shape[0] // 2
    return jnp.where(iota((half, stack.shape[1]), 1) < HEAD_DIM, stack[:half], stack[half:])


def normalized(hidden):
    center = hidden - jnp.mean(hidden, axis=-1, keepdims=True)
    spread_of = jnp.mean(center * center, axis=-1, keepdims=True)
    inverse = lax.rsqrt(spread_of + EPSILON)
    return center * inverse, inverse


def norm_back(scaled, unit, inverse):
    return inverse * (
        scaled
        - jnp.mean(scaled, axis=-1, keepdims=True)
        - unit * jnp.mean(scaled * unit, axis=-1, keepdims=True)
    )


def segments(dims):
    short_rows, long_count, long_length, _ = dims
    return [(0, short_rows, None)] + [
        (short_rows + i * long_length, long_length, i) for i in range(long_count)
    ]


def key_bias(slen, llen, short_length, rows, long_at):
    key = iota((rows, rows), 0)
    if long_at is not None:
        return jnp.where(key < llen[long_at], 0.0, -1e9).astype(F32)
    query = iota((rows, rows), 1)
    keep = jnp.zeros((rows, rows), jnp.bool_)
    for p in range(rows // short_length):
        low, high = p * short_length, (p + 1) * short_length
        keep = keep | ((key >= low) & (key < low + slen[p]) & (query >= low) & (query < high))
    return jnp.where(keep, 0.0, -1e9).astype(F32)


def valid_rows(slen, llen, dims):
    short_rows, long_count, long_length, short_length = dims
    parts = []
    at = iota((short_length, 1), 0)
    for p in range(short_rows // short_length):
        parts.append((at < slen[p]).astype(F32))
    at = iota((long_length, 1), 0)
    for p in range(long_count):
        parts.append((at < llen[p]).astype(F32))
    return jnp.concatenate(parts, axis=0)


def pack_body(wqkv, wo, wup, wdown, *rest):
    vectors, out = rest[:-1], rest[-1]
    each, width = wo.shape
    slabs = wqkv.shape[1] // width
    for j in range(slabs):
        out[j * each : (j + 1) * each] = wqkv[:, j * width : (j + 1) * width]
    out[slabs * each : (slabs + 1) * each] = wo[...]
    base = (slabs + 1) * each
    slabs = wup.shape[1] // width
    for j in range(slabs):
        out[base + j * each : base + (j + 1) * each] = wup[:, j * width : (j + 1) * width]
    base += slabs * each
    out[base : base + wdown.shape[0]] = wdown[...]
    base += wdown.shape[0]
    out[base:] = jnp.zeros((8, width), BF16)
    for i, v in enumerate(vectors[:-1]):
        out[base : base + 1, i * each : (i + 1) * each] = v[...]
    out[base + 1 : base + 2, : vectors[-1].shape[1]] = vectors[-1][...]


def pack(wqkv, wo, wup, wdown, vectors, ub):
    each, width = wo.shape
    rows = each * (wqkv.shape[1] // width + 1 + wup.shape[1] // width) + wdown.shape[0] + 8
    return pl.pallas_call(
        pack_body,
        out_shape=jax.ShapeDtypeStruct((rows, width), BF16),
        compiler_params=params(),
        name="pack",
    )(wqkv, wo, wup, wdown, *[v[None] for v in vectors], ub[None])


def attention_forward_body(
    dims, slen, llen, xs, xl, wq, wk, wv, wo_block, small,
    q_o, k_o, v_o, c_o, ps_o, pl_o, n_o, r_o, low_o, vecs_o, ub_o,
    x_all, total, wo_all,
):
    step = pl.program_id(0)
    short_rows, width = dims[0], x_all.shape[1]
    cols = q_o.shape[1]

    @pl.when(step == 0)
    def _():
        x_all[:short_rows, :] = xs[...]
        x_all[short_rows:, :] = xl[...]
        total[...] = jnp.zeros_like(total)
        wo_all[...] = wo_block[...].reshape(width, width)
        packed = small[...]
        each = width // SHARDS
        line = packed[:, 0, : 8 * each + 64]
        rest = column_rest(line.shape[1], width, each)
        mine = spread(SHARDS, width)
        for i in range(8):
            pick = (iota(rest.shape, 0) == rest + i * each).astype(BF16)
            row = jnp.sum(jnp.where(mine, nn(line, pick), 0.0), axis=0, keepdims=True)
            vecs_o[i : i + 1] = row.astype(BF16)
        inner = ub_o.shape[1]
        line = packed[:, 1, :128]
        pick = (iota((128, inner), 0) == column_rest(128, inner, inner // SHARDS)).astype(BF16)
        row = jnp.sum(jnp.where(spread(SHARDS, inner), nn(line, pick), 0.0), axis=0, keepdims=True)
        ub_o[...] = row.astype(BF16)

    x = x_all[...]
    at_cols = pl.ds(pl.multiple_of(step * cols, cols), cols)
    q_o[...] = (nn(x, wq[...].reshape(width, cols)) + vecs_o[QB : QB + 1, at_cols].astype(F32)).astype(BF16)
    k_o[...] = nn(x, wk[...].reshape(width, cols)).astype(BF16)
    v_o[...] = (nn(x, wv[...].reshape(width, cols)) + vecs_o[VB : VB + 1, at_cols].astype(F32)).astype(BF16)
    for first, rows, long_at in segments(dims):
        bias = key_bias(slen, llen, dims[3], rows, long_at)
        at = slice(first, first + rows)
        for pair in range(cols // PAIR):
            lanes = slice(pair * PAIR, (pair + 1) * PAIR)
            q = q_o[at, lanes] * jnp.asarray(HEAD_DIM**-0.5, BF16)
            scores = nt(two_heads(k_o[at, lanes]), q)
            probs = []
            for h in range(2):
                s = scores[h * rows : (h + 1) * rows] + bias
                e = jnp.exp(s - jnp.max(s, axis=0, keepdims=True))
                probs.append((e * (1.0 / jnp.sum(e, axis=0, keepdims=True))).astype(BF16))
            probs = jnp.concatenate(probs, axis=0)
            if long_at is None:
                ps_o[pair] = probs
            else:
                pl_o[long_at, pair] = probs
            c_o[at, lanes] = tn(two_heads(v_o[at, lanes]), probs).T.astype(BF16)
    total[...] += nn(c_o[...], wo_all[at_cols, :])

    @pl.when(step == pl.num_programs(0) - 1)
    def _():
        h = x_all[...].astype(F32) + (total[...] + row_of(vecs_o, OB))
        unit, inverse = normalized(h)
        n_o[...] = unit
        r_o[...] = inverse
        low_o[...] = (unit * row_of(vecs_o, G1) + row_of(vecs_o, S1)).astype(BF16)


def attention_forward(slen, llen, xs, xl, gathered, inner, dims):
    rows, width = xs.shape[0] + xl.shape[0], xs.shape[1]
    short_rows, long_count, long_length, _ = dims
    each = width // SHARDS
    step = 256
    steps, pairs = width // step, width // PAIR
    per = step // PAIR
    slab = lambda i: pl.BlockSpec((SHARDS, each, step), lambda g, *_: (0, i, g))
    cols = pl.BlockSpec((rows, step), lambda g, *_: (0, g))
    return pl.pallas_call(
        functools.partial(attention_forward_body, dims),
        grid_spec=pltpu.PrefetchScalarGridSpec(
            num_scalar_prefetch=2,
            grid=(steps,),
            in_specs=[
                whole(*xs.shape), whole(*xl.shape), slab(0), slab(1), slab(2),
                pl.BlockSpec((SHARDS, each, width), lambda g, *_: (0, 3, 0)),
                pl.BlockSpec((SHARDS, 8, width), lambda g, *_: (0, gathered.shape[1] // 8 - 1, 0)),
            ],
            out_specs=[
                cols, cols, cols, cols,
                pl.BlockSpec((per, 2 * short_rows, short_rows), lambda g, *_: (g, 0, 0)),
                pl.BlockSpec((long_count, per, 2 * long_length, long_length), lambda g, *_: (0, g, 0, 0)),
                whole(rows, width), whole(rows, 1), whole(rows, width), whole(8, width), whole(1, inner),
            ],
            scratch_shapes=[
                pltpu.VMEM((rows, width), BF16), pltpu.VMEM((rows, width), F32), pltpu.VMEM((width, width), BF16),
            ],
        ),
        out_shape=[
            *[jax.ShapeDtypeStruct((rows, width), BF16)] * 4,
            jax.ShapeDtypeStruct((pairs, 2 * short_rows, short_rows), BF16),
            jax.ShapeDtypeStruct((long_count, pairs, 2 * long_length, long_length), BF16),
            jax.ShapeDtypeStruct((rows, width), F32),
            jax.ShapeDtypeStruct((rows, 1), F32),
            jax.ShapeDtypeStruct((rows, width), BF16),
            jax.ShapeDtypeStruct((8, width), BF16),
            jax.ShapeDtypeStruct((1, inner), BF16),
        ],
        compiler_params=params(),
        cost_estimate=cost(8 * rows * width * width, 20e6),
        name="attention_forward",
    )(slen, llen, xs, xl, gathered, gathered, gathered, gathered, gathered)


def feed_forward_body(
    dims, half,
    slen, llen, pos, low, unit1, cot_s, cot_l, wup, ub, wdown, vecs,
    gelu_o, keep, give, gffn_o, gss_o, outs_o, outl_o, sums_o,
    hidden, total,
):
    step = pl.program_id(0)
    short_rows = dims[0]
    block, width = hidden.shape[2], low.shape[1]

    @pl.when(step < half)
    def _():
        pre = nn(low[...], wup[...].reshape(width, block)) + ub[...].astype(F32)
        cdf = 0.5 + 0.5 * lax.erf(pre * (0.5**0.5))
        density = jnp.exp(-0.5 * pre * pre) * (0.5 / jnp.pi) ** 0.5
        h = (pre * cdf).astype(BF16)
        gelu_o[...] = (cdf + pre * density).astype(BF16)
        hidden[step] = h
        part = nn(h, wdown[...].reshape(block, width))

        @pl.when(step == 0)
        def _():
            total[...] = part

        @pl.when(step > 0)
        def _():
            total[...] += part

    @pl.when(step == half - 1)
    def _():
        first = unit1[...] * row_of(vecs, G1) + row_of(vecs, S1)
        unit, inverse = normalized(first + (total[...] + row_of(vecs, DB)))
        valid = valid_rows(slen, llen, dims)
        out = ((unit * row_of(vecs, G2) + row_of(vecs, S2)) * valid).astype(BF16)
        outs_o[...] = out[:short_rows]
        outl_o[...] = out[short_rows:]
        cot = jnp.concatenate([cot_s[...], cot_l[...]], axis=0).astype(F32) * valid
        back = norm_back(cot * row_of(vecs, G2), unit, inverse)
        gss_o[...] = back
        low_back = back.astype(BF16)
        gffn_o[...] = low_back
        sums_o[...] = jnp.zeros_like(sums_o)
        sums_o[DB : DB + 1] = jnp.sum(low_back.astype(F32), axis=0, keepdims=True)
        sums_o[G2 : G2 + 1] = jnp.sum(cot * unit, axis=0, keepdims=True)
        sums_o[S2 : S2 + 1] = jnp.sum(cot, axis=0, keepdims=True)

    @pl.when(step >= half)
    def _():
        x = step - half
        grad = tn(hidden[x], gffn_o[...]).astype(BF16)
        each = block // (2 * RING)
        first = pos[2] == 0
        for z in range(RING):
            p0, p1 = places(pos, x, z)
            even, odd = grad[2 * z * each : (2 * z + 1) * each], grad[(2 * z + 1) * each : (2 * z + 2) * each]
            keep[jnp.where(first, p0, p1)] = jnp.where(first, even, odd)
            give[jnp.where(first, p1, p0)] = jnp.where(first, odd, even)


def feed_forward(slen, llen, pos, low, unit1, cot_s, cot_l, gathered, ub, vecs, dims):
    rows, width = low.shape
    inner = ub.shape[1]
    half = RING
    block = inner // half
    each, tall = width // SHARDS, inner // SHARDS
    step_of = lambda g: jnp.minimum(g, half - 1)
    cols = lambda r: pl.BlockSpec((r, block), lambda g, *_: (0, step_of(g)))
    return pl.pallas_call(
        functools.partial(feed_forward_body, dims, half),
        grid_spec=pltpu.PrefetchScalarGridSpec(
            num_scalar_prefetch=3,
            grid=(2 * half,),
            in_specs=[
                whole(rows, width), whole(rows, width), whole(*cot_s.shape), whole(*cot_l.shape),
                pl.BlockSpec((SHARDS, each, width), lambda g, *_: (0, 4 + step_of(g), 0)),
                cols(1),
                pl.BlockSpec((SHARDS // half, tall, width), lambda g, *_: (step_of(g), 8 * each // tall, 0)),
                whole(*vecs.shape),
            ],
            out_specs=[
                cols(rows),
                whole(CHIPS, tall, width), whole(CHIPS, tall, width),
                whole(rows, width), whole(rows, width), whole(*cot_s.shape), whole(*cot_l.shape),
                whole(8, width),
            ],
            scratch_shapes=[pltpu.VMEM((half, rows, block), BF16), pltpu.VMEM((rows, width), F32)],
        ),
        out_shape=[
            jax.ShapeDtypeStruct((rows, inner), BF16),
            jax.ShapeDtypeStruct((CHIPS, tall, width), BF16),
            jax.ShapeDtypeStruct((CHIPS, tall, width), BF16),
            jax.ShapeDtypeStruct((rows, width), BF16),
            jax.ShapeDtypeStruct((rows, width), F32),
            jax.ShapeDtypeStruct(cot_s.shape, BF16),
            jax.ShapeDtypeStruct(cot_l.shape, BF16),
            jax.ShapeDtypeStruct((8, width), F32),
        ],
        compiler_params=params(),
        cost_estimate=cost(6 * rows * width * inner, 30e6),
        name="feed_forward",
    )(slen, llen, pos, low, unit1, cot_s, cot_l, gathered, ub, gathered, vecs)


def feed_back_body(
    pos, gffn, gss, gelu, wdown, wup, low, unit1, inv1, vecs,
    keep, give, dub_o, gfs_o, gatt_o, sums_o,
    total,
):
    step = pl.program_id(0)
    width, block = low.shape[1], gelu.shape[1]
    up = (nt(gffn[...], wdown[...].reshape(block, width)) * gelu[...].astype(F32)).astype(BF16)
    dub_o[...] = jnp.sum(up.astype(F32), axis=0, keepdims=True)
    deal(keep, give, pos, tn(low[...], up).astype(BF16), slice(None), width // SHARDS)
    part = nt(up, wup[...].reshape(width, block))

    @pl.when(step == 0)
    def _():
        total[...] = part

    @pl.when(step > 0)
    def _():
        total[...] += part

    @pl.when(step == pl.num_programs(0) - 1)
    def _():
        grad = gss[...] + total[...]
        unit = unit1[...]
        back = norm_back(grad * row_of(vecs, G1), unit, inv1[...])
        gfs_o[...] = back
        low_back = back.astype(BF16)
        gatt_o[...] = low_back
        sums_o[...] = jnp.zeros_like(sums_o)
        sums_o[OB : OB + 1] = jnp.sum(low_back.astype(F32), axis=0, keepdims=True)
        sums_o[G1 : G1 + 1] = jnp.sum(grad * unit, axis=0, keepdims=True)
        sums_o[S1 : S1 + 1] = jnp.sum(grad, axis=0, keepdims=True)


def feed_back(pos, gffn, gss, gelu, gathered, low, unit1, inv1, vecs):
    rows, width = low.shape
    inner = gelu.shape[1]
    half = RING
    block = inner // half
    each, tall = width // SHARDS, inner // SHARDS
    cols = lambda r: pl.BlockSpec((r, block), lambda g, *_: (0, g))
    dealt = pl.BlockSpec((CHIPS, each, width), lambda g, *_: (0, g, 0))
    return pl.pallas_call(
        feed_back_body,
        grid_spec=pltpu.PrefetchScalarGridSpec(
            num_scalar_prefetch=1,
            grid=(half,),
            in_specs=[
                whole(rows, width), whole(rows, width), cols(rows),
                pl.BlockSpec((SHARDS // half, tall, width), lambda g, *_: (g, 8 * each // tall, 0)),
                pl.BlockSpec((SHARDS, each, width), lambda g, *_: (0, 4 + g, 0)),
                whole(rows, width), whole(rows, width), whole(rows, 1), whole(*vecs.shape),
            ],
            out_specs=[dealt, dealt, cols(1), whole(rows, width), whole(rows, width), whole(8, width)],
            scratch_shapes=[pltpu.VMEM((rows, width), F32)],
        ),
        out_shape=[
            jax.ShapeDtypeStruct((CHIPS, tall, width), BF16),
            jax.ShapeDtypeStruct((CHIPS, tall, width), BF16),
            jax.ShapeDtypeStruct((1, inner), F32),
            jax.ShapeDtypeStruct((rows, width), F32),
            jax.ShapeDtypeStruct((rows, width), BF16),
            jax.ShapeDtypeStruct((8, width), F32),
        ],
        compiler_params=params(),
        cost_estimate=cost(6 * rows * width * inner, 25e6),
        name="feed_back",
    )(pos, gffn, gss, gelu, gathered, gathered, low, unit1, inv1, vecs)


def attention_back_body(
    dims,
    pos, gatt, gatt_cols, wo_block, c, q, k, v, ps, plong, xs, xl, sums_f, sums_b, dub,
    keep, give, dq_o, dk_o, dv_o,
    x_all, gc, wo_all, sums,
):
    step = pl.program_id(0)
    short_rows, width = dims[0], x_all.shape[1]
    cols = q.shape[1]
    each = width // SHARDS
    at_cols = pl.ds(pl.multiple_of(step * cols, cols), cols)

    @pl.when(step == 0)
    def _():
        x_all[:short_rows, :] = xs[...]
        x_all[short_rows:, :] = xl[...]
        wo_all[...] = wo_block[...].reshape(width, width)
        sums[...] = sums_f[...] + sums_b[...]

    deal(keep, give, pos, tn(c[...], gatt_cols[...]).astype(BF16), slice(3 * each, 4 * each), each)
    gc[...] = nt(gatt[...], wo_all[at_cols, :]).astype(BF16)
    scale = HEAD_DIM**-0.5
    for first, rows, long_at in segments(dims):
        at = slice(first, first + rows)
        for pair in range(cols // PAIR):
            lanes = slice(pair * PAIR, (pair + 1) * PAIR)
            probs = ps[pair] if long_at is None else plong[long_at, pair]
            grad = gc[at, lanes]
            dp = nt(two_heads(v[at, lanes]), grad)
            ds = []
            for h in range(2):
                half = slice(h * rows, (h + 1) * rows)
                p = probs[half].astype(F32)
                d = dp[half]
                ds.append((p * (d - jnp.sum(d * p, axis=0, keepdims=True))).astype(BF16))
            ds = jnp.concatenate(ds, axis=0)
            dv_o[at, lanes] = own_lanes(nn(probs, grad)).astype(BF16)
            dk_o[at, lanes] = (own_lanes(nn(ds, q[at, lanes])) * scale).astype(BF16)
            dq_o[at, lanes] = (tn(two_heads(k[at, lanes]), ds).T * scale).astype(BF16)
    x = x_all[...]
    for i, d in enumerate((dq_o, dk_o, dv_o)):
        deal(keep, give, pos, tn(x, d[...]).astype(BF16), slice(i * each, (i + 1) * each), each)
    sums[QB : QB + 1, at_cols] = jnp.sum(dq_o[...].astype(F32), axis=0, keepdims=True)
    sums[VB : VB + 1, at_cols] = jnp.sum(dv_o[...].astype(F32), axis=0, keepdims=True)
    keep[:, 4 * each :] = jnp.zeros((CHIPS, 8, cols), BF16)
    give[:, 4 * each :] = jnp.zeros((CHIPS, 8, cols), BF16)

    @pl.when(step == pl.num_programs(0) - 1)
    def _():
        mine = spread(SHARDS, width)
        rest = column_rest(cols, width, each)
        line = jnp.zeros((SHARDS, cols), F32)
        for i in range(8):
            put = (iota(rest.shape, 0) == rest + i * each).astype(BF16)
            line += nt(jnp.where(mine, sums[i : i + 1], 0.0).astype(BF16), put)
        inner = dub.shape[1]
        put = (iota((cols, inner), 0) == column_rest(cols, inner, inner // SHARDS)).astype(BF16)
        wide = nt(jnp.where(spread(SHARDS, inner), dub[...], 0.0).astype(BF16), put)
        both = jnp.concatenate([line[:, None], wide[:, None], jnp.zeros((SHARDS, 6, cols), F32)], axis=1)
        deal(keep, give, pos, both.reshape(SHARDS * 8, cols).astype(BF16), slice(4 * each, 4 * each + 8), 8)


def attention_back(pos, gatt, gathered, c, q, k, v, ps, plong, xs, xl, sums_f, sums_b, dub, dims):
    rows, width = gatt.shape
    short_rows, long_count, long_length, _ = dims
    each = width // SHARDS
    step = 256
    per = step // PAIR
    cols = pl.BlockSpec((rows, step), lambda g, *_: (0, g))
    dealt = pl.BlockSpec((CHIPS, 4 * each + 8, step), lambda g, *_: (0, 0, g))
    return pl.pallas_call(
        functools.partial(attention_back_body, dims),
        grid_spec=pltpu.PrefetchScalarGridSpec(
            num_scalar_prefetch=1,
            grid=(width // step,),
            in_specs=[
                whole(rows, width), cols,
                pl.BlockSpec((SHARDS, each, width), lambda g, *_: (0, 3, 0)),
                whole(rows, width), cols, cols, cols,
                pl.BlockSpec((per, 2 * short_rows, short_rows), lambda g, *_: (g, 0, 0)),
                pl.BlockSpec((long_count, per, 2 * long_length, long_length), lambda g, *_: (0, g, 0, 0)),
                whole(*xs.shape), whole(*xl.shape), whole(8, width), whole(8, width), whole(*dub.shape),
            ],
            out_specs=[dealt, dealt, cols, cols, cols],
            scratch_shapes=[
                pltpu.VMEM((rows, width), BF16), pltpu.VMEM((rows, step), BF16),
                pltpu.VMEM((width, width), BF16), pltpu.VMEM((8, width), F32),
            ],
        ),
        out_shape=[
            *[jax.ShapeDtypeStruct((CHIPS, 4 * each + 8, width), BF16)] * 2,
            *[jax.ShapeDtypeStruct((rows, width), BF16)] * 3,
        ],
        compiler_params=params(),
        cost_estimate=cost(12 * rows * width * width, 25e6),
        name="attention_back",
    )(pos, gatt, gatt, gathered, c, q, k, v, ps, plong, xs, xl, sums_f, sums_b, dub)


def input_back_body(dims, gfs, dq, dk, dv, wq, wk, wv, gs_o, gl_o, total):
    step = pl.program_id(0)
    short_rows, width, cols = dims[0], gfs.shape[1], dq.shape[1]
    part = (
        nt(dq[...], wq[...].reshape(width, cols))
        + nt(dk[...], wk[...].reshape(width, cols))
        + nt(dv[...], wv[...].reshape(width, cols))
    )

    @pl.when(step == 0)
    def _():
        total[...] = gfs[...] + part

    @pl.when(step > 0)
    def _():
        total[...] += part

    @pl.when(step == pl.num_programs(0) - 1)
    def _():
        gs_o[...] = total[:short_rows]
        gl_o[...] = total[short_rows:]


def input_back(gfs, dq, dk, dv, gathered, dims):
    rows, width = gfs.shape
    each = width // SHARDS
    step = 256
    short_rows = dims[0]
    cols = pl.BlockSpec((rows, step), lambda g: (0, g))
    slab = lambda i: pl.BlockSpec((SHARDS, each, step), lambda g: (0, i, g))
    return pl.pallas_call(
        functools.partial(input_back_body, dims),
        grid=(width // step,),
        in_specs=[whole(rows, width), cols, cols, cols, slab(0), slab(1), slab(2)],
        out_specs=[whole(short_rows, width), whole(rows - short_rows, width)],
        scratch_shapes=[pltpu.VMEM((rows, width), F32)],
        out_shape=[
            jax.ShapeDtypeStruct((short_rows, width), F32),
            jax.ShapeDtypeStruct((rows - short_rows, width), F32),
        ],
        compiler_params=params(),
        cost_estimate=cost(6 * rows * width * width, 12e6),
        name="input_back",
    )(gfs, dq, dk, dv, gathered, gathered, gathered)


def pair_sum_body(keep, got, *outs):
    for i, o in enumerate(outs):
        at = slice(i * RING, (i + 1) * RING)
        o[...] = (keep[at].astype(F32) + got[at].astype(F32)).astype(BF16)


def ring_sum_body(own, left, right, far, *outs):
    total = (own[...].astype(F32) + far[...].astype(F32)) + (left[...].astype(F32) + right[...].astype(F32))
    if len(outs) == 1:
        outs[0][...] = total.astype(BF16)
    else:
        for i, o in enumerate(outs):
            o[...] = total[i].astype(BF16)


def turn(delta, stage):
    moves = []
    for x in range(RING):
        for z in range(RING):
            for core in range(2):
                to_x, to_z = x, z
                if (core == 0) == (stage == 0):
                    to_x = (x + delta) % RING
                else:
                    to_z = (z + delta) % RING
                moves.append(((x * RING + z) * 2 + core, (to_x * RING + to_z) * 2 + core))
    return moves


def swap_cores(v):
    return lax.ppermute(v, "shard", [(i, i ^ 1) for i in range(SHARDS)])


def to_owner(keep, give):
    got = swap_cores(give)
    rows, width = keep.shape[1:]
    quarter = jax.ShapeDtypeStruct((RING, rows, width), BF16)
    parts = pl.pallas_call(
        pair_sum_body, out_shape=[quarter] * RING, compiler_params=params(), name="pair_sum",
        cost_estimate=cost(keep.size, 6 * keep.size),
    )(keep, got)
    left, far, right = (lax.ppermute(parts[d], "shard", turn(d, 0)) for d in (1, 2, 3))
    block = jax.ShapeDtypeStruct((rows, width), BF16)
    parts = pl.pallas_call(
        ring_sum_body, out_shape=[block] * RING, compiler_params=params(), name="ring_sum",
        cost_estimate=cost(4 * RING * rows * width, 10 * RING * rows * width),
    )(parts[0], left, right, far)
    left, far, right = (lax.ppermute(parts[d], "shard", turn(d, 1)) for d in (1, 2, 3))
    own = pl.pallas_call(
        ring_sum_body, out_shape=[block], compiler_params=params(), name="ring_sum",
        cost_estimate=cost(4 * rows * width, 10 * rows * width),
    )(parts[0], left, right, far)[0]
    return own, *(lax.ppermute(own, "rep", [(i, (i + d) % RING) for i in range(RING)]) for d in (1, 3, 2))


def replica_sum(own, left, right, far, at):
    return (own[at].astype(F32) + far[at].astype(F32)) + (left[at].astype(F32) + right[at].astype(F32))


def finish_attention_body(own, left, right, far, wqkv_o, wo_o, *vector_os):
    each, width = wo_o.shape
    for j in range(wqkv_o.shape[1] // width):
        at = slice(j * each, (j + 1) * each)
        wqkv_o[:, j * width : (j + 1) * width] = replica_sum(own, left, right, far, at)
    wo_o[...] = replica_sum(own, left, right, far, slice(3 * each, 4 * each))
    last = replica_sum(own, left, right, far, slice(4 * each, 4 * each + 8))[:, width - 256 :]
    for i, o in enumerate(vector_os[:-1]):
        o[...] = last[0:1, i * each : (i + 1) * each]
    o = vector_os[-1]
    o[...] = last[1:2, : o.shape[1]]


def finish_attention(arrays, tall):
    width = arrays[0].shape[1]
    each = width // SHARDS
    return pl.pallas_call(
        finish_attention_body,
        out_shape=[
            jax.ShapeDtypeStruct((each, 3 * width), F32),
            jax.ShapeDtypeStruct((each, width), F32),
            *[jax.ShapeDtypeStruct((1, each), F32)] * 8,
            jax.ShapeDtypeStruct((1, tall), F32),
        ],
        compiler_params=params(),
        name="finish_attention",
    )(*arrays)


def finish_feed_body(own, left, right, far, out):
    each, wide = out.shape
    width = own.shape[1]
    for j in range(wide // width):
        at = slice(j * each, (j + 1) * each)
        out[:, j * width : (j + 1) * width] = replica_sum(own, left, right, far, at)


def finish_feed(arrays, shape):
    return pl.pallas_call(
        finish_feed_body,
        out_shape=jax.ShapeDtypeStruct(shape, F32),
        compiler_params=params(),
        name="finish_feed",
    )(*arrays)


def on_device(
    short_tokens, long_tokens, short_lengths, long_lengths, short_cotangent, long_cotangent,
    input_weight, query_bias, value_bias, output_weight, output_bias, first_gain, first_shift,
    up_weight, up_bias, down_weight, down_bias, second_gain, second_shift,
):
    short_count, short_length, width = short_tokens.shape
    long_count, long_length, _ = long_tokens.shape
    dims = (short_count * short_length, long_count, long_length, short_length)
    each, inner, tall = width // SHARDS, up_weight.shape[1], down_weight.shape[0]
    xs, xl = short_tokens.reshape(-1, width), long_tokens.reshape(-1, width)
    cs, cl = short_cotangent.reshape(-1, width), long_cotangent.reshape(-1, width)
    index = lax.axis_index("shard")
    pos = jnp.stack([index // 8, (index // 2) % 4, index % 2]).astype(jnp.int32)

    packed = pack(
        input_weight, output_weight, up_weight, down_weight,
        (query_bias, value_bias, output_bias, first_gain, first_shift, down_bias, second_gain, second_shift),
        up_bias,
    )
    gathered = lax.all_gather(packed, "shard", axis=0)
    q, k, v, c, ps, plong, unit1, inv1, low, vecs, ub = attention_forward(
        short_lengths, long_lengths, xs, xl, gathered, inner, dims
    )
    gelu, keep_d, give_d, gffn, gss, out_s, out_l, sums_f = feed_forward(
        short_lengths, long_lengths, pos, low, unit1, cs, cl, gathered, ub, vecs, dims
    )
    down = finish_feed(to_owner(keep_d, give_d), (tall, width))
    keep_u, give_u, dub, gfs, gatt, sums_b = feed_back(pos, gffn, gss, gelu, gathered, low, unit1, inv1, vecs)
    up = finish_feed(to_owner(keep_u, give_u), (each, inner))
    keep_a, give_a, dq, dk, dv = attention_back(
        pos, gatt, gathered, c, q, k, v, ps, plong, xs, xl, sums_f, sums_b, dub, dims
    )
    w_in, w_out, *vectors = finish_attention(to_owner(keep_a, give_a), tall)
    grad_s, grad_l = input_back(gfs, dq, dk, dv, gathered, dims)
    vectors = [x.reshape(-1) for x in vectors]
    return (
        out_s.reshape(short_tokens.shape), out_l.reshape(long_tokens.shape),
        grad_s.reshape(short_tokens.shape), grad_l.reshape(long_tokens.shape),
        w_in, vectors[QB], vectors[VB], w_out, vectors[OB], vectors[G1], vectors[S1],
        up, vectors[8], down, vectors[DB], vectors[G2], vectors[S2],
    )


def solution(mesh):
    rows, flat = P(("rep", "shard"), None, None), P("shard")
    tall = P("shard", None)
    return jax.shard_map(
        on_device,
        mesh=mesh,
        in_specs=(
            rows, rows, P(("rep", "shard")), P(("rep", "shard")), rows, rows,
            tall, flat, flat, tall, flat, flat, flat, tall, flat, tall, flat, flat, flat,
        ),
        out_specs=(
            rows, rows, rows, rows,
            tall, flat, flat, tall, flat, flat, flat, tall, flat, tall, flat, flat, flat,
        ),
        check_vma=False,
    )
```

time: 617 us -> 275 us (0.45)
  the two profiles are of different devices: /device:TPU:0 before, /device:TPU:6 now
where the time goes in v1:
time: 275 us
  Pallas kernels  122 us (44%)
  waiting for transfers between devices  93 us (34%)
  starting transfers between devices  37.6 us (14%)
  between operations  14.3 us (5%)
  local copies, waits for them, and re-layouts  7.84 us (3%)
    all_gather x1, waiting for transfers between devices, on_device(): gathered = lax.all_gather(packed, 'shard', axis=0)  71 us
    pallas_call x1, Pallas kernels, feed_forward(): pl.pallas_call(functools.partial(feed_forward_body, dims, half), grid_spe...  23.9 us
    pallas_call x1, Pallas kernels, attention_back(): pl.pallas_call(functools.partial(attention_back_body, dims), grid_spec=pl...  19.8 us
    pallas_call x1, Pallas kernels, feed_back(): pl.pallas_call(feed_back_body, grid_spec=pltpu.PrefetchScalarGridSpec(num...  19.3 us
    ppermute x9, waiting for transfers between devices, to_owner(): lax.ppermute(parts[d], 'shard', turn(d, 0))  19 us
    pallas_call x1, Pallas kernels, attention_forward(): pl.pallas_call(functools.partial(attention_forward_body, dims), grid_spec...  17.6 us
    ppermute x9, starting transfers between devices, to_owner(): lax.ppermute(own, 'rep', [(i, (i + d) % RING) for i in range(RING)])  12.6 us
    pallas_call x3, Pallas kernels, to_owner(): pl.pallas_call(pair_sum_body, out_shape=[quarter] * RING, compiler_params...  12 us
  transfers between devices with their start and end apart: 31, of which 6 were waited for; matrix products, arithmetic and copies ran while one was open for 0% of the time, Pallas kernels for 28%

profile of v1, /device:TPU:6, one launch (start us, length us, event | category | flops | bytes accessed | tf_op | source)
XLA Modules:
  0.0 274.9 jit_solution(10090450752099213667)
XLA Ops:
  7.2 0.0 all-gather.3.cloned.1.call-start
  7.2 2.0 pack.1
  9.3 0.0 all-gather.3.cloned.1.call-update
  9.3 0.6 pad_add_fusion.pos
  9.9 71.0 %all-gather.3.cloned.1.call-done = bf16[9472,768]{1,0:T(8,128)(2,1)} async-done(((bf16[296,768]{1,0:T(8,128)(2,1)}), bf16[9472,768]{1,0:T(8,128)(2,1)}) %all-gather.3.cloned.1.call-update) | async-done | bytes 14549008 | tf_op jit(solution)/shard_map/all_gather | solution.py:721
  80.9 17.6 %attention_forward.1 = (bf16[640,768]{1,0:T(8,128)(2,1)}, bf16[640,768]{1,0:T(8,128)(2,1)}, bf16[640,768]{1,0:T(8,128)(2,1)}, bf16[640,768]{1,0:T(8,128)(2,1)}, ...) custom-call(s32[2]{0:T(128)} %slen.3, s32[2]{0:T(128)} %llen.3, ...), custom_call_target="tpu_custom_call" | custom-call | flops 3019898880 | bytes 20000000 | tf_op jit(solution)/shard_map/attention_forward/pallas_call | solution.py:243
  98.5 23.9 %feed_forward.1 = (bf16[640,3072]{1,0:T(8,128)(2,1)}, bf16[16,96,768]{2,1,0:T(8,128)(2,1)}, bf16[16,96,768]{2,1,0:T(8,128)(2,1)}, bf16[640,768]{1,0:T(8,128)(2,1...) custom-call(s32[2]{0:T(128)} %slen.3, s32[2]{0:T(128)} %llen.3, ...), custom_call_target="tpu_custom_call" | custom-call | flops 9059696640 | bytes 30000000 | tf_op jit(solution)/shard_map/feed_forward/pallas_call | solution.py:346
  122.5 0.5 collective-permute-start.20
  123.0 19.3 %feed_back.1 = (bf16[16,96,768]{2,1,0:T(8,128)(2,1)}, bf16[16,96,768]{2,1,0:T(8,128)(2,1)}, f32[1,3072]{1,0:T(1,128)}, f32[640,768]{1,0:T(8,128)}, bf16[640,768]{1,0:T(8,128)(2,1)}, /*index=5*/f32[8,768]{1,0:T(8,128)}) custom-call(s32[3]{0:T(128)} %pad_add_fusion.pos, bf16[640,768]{1,0:T(8,128)(2,1)} %get-tuple-element.90.gffn, ...), custom_call_target="tpu_custom_call" | custom-call | flops 9059696640 | bytes 25000000 | tf_op jit(solution)/shard_map/feed_back/pallas_call | solution.py:424
  142.4 0.3 collective-permute-start.10
  142.7 19.8 %attention_back.1 = (bf16[16,104,768]{2,1,0:T(8,128)(2,1)}, bf16[16,104,768]{2,1,0:T(8,128)(2,1)}, bf16[640,768]{1,0:T(8,128)(2,1)}, bf16[640,768]{1,0:T(8,128)(2,1)}, bf16[640,768]{1,0:T(8,128)(2,1)}) custom-call(s32[3]{0:T(128)} %pad_add_fusion.pos, bf16[640,768]{1,0:T(8,128)(2,1)} %get-tuple-element.95.gatt.gatt_cols, ...), custom_call_target="tpu_custom_call" | custom-call | flops 4529848320 | bytes 25000000 | tf_op jit(solution)/shard_map/attention_back/pallas_call | solution.py:522
  162.5 0.3 collective-permute-start
  162.8 1.4 copy-done.2
  164.2 4.0 %pair_sum.5 = (bf16[4,96,768]{2,1,0:T(8,128)(2,1)}, bf16[4,96,768]{2,1,0:T(8,128)(2,1)}, bf16[4,96,768]{2,1,0:T(8,128)(2,1)}, bf16[4,96,768]{2,1,0:T(8,128)(2,1)}) custom-call(bf16[16,96,768]{2,1,0:T(8,128)(2,1)} %get-tuple-element.138.keep, bf16[16,96,768]{2,1,0:T(8,128)(2,1)} %copy-done.2), custom_call_target="tpu_custom_call" | custom-call | flops 1179648 | bytes 7077888 | tf_op jit(solution)/shard_map/pair_sum/pallas_call | solution.py:634
  168.2 0.5 collective-permute-start.21
  168.7 1.5 collective-permute-start.22
  170.2 1.5 collective-permute-start.23
  171.7 1.4 copy-done.1
  173.1 4.0 %pair_sum.4 = (bf16[4,96,768]{2,1,0:T(8,128)(2,1)}, bf16[4,96,768]{2,1,0:T(8,128)(2,1)}, bf16[4,96,768]{2,1,0:T(8,128)(2,1)}, bf16[4,96,768]{2,1,0:T(8,128)(2,1)}) custom-call(bf16[16,96,768]{2,1,0:T(8,128)(2,1)} %get-tuple-element.127.keep, bf16[16,96,768]{2,1,0:T(8,128)(2,1)} %copy-done.1), custom_call_target="tpu_custom_call" | custom-call | flops 1179648 | bytes 7077888 | tf_op jit(solution)/shard_map/pair_sum/pallas_call | solution.py:634
  177.1 2.1 collective-permute-start.11
  179.2 0.0 collective-permute-done.got
  179.2 1.4 copy-done
  180.6 4.1 %pair_sum.3 = (bf16[4,104,768]{2,1,0:T(8,128)(2,1)}, bf16[4,104,768]{2,1,0:T(8,128)(2,1)}, bf16[4,104,768]{2,1,0:T(8,128)(2,1)}, bf16[4,104,768]{2,1,0:T(8,128)(2,1)}) custom-call(bf16[16,104,768]{2,1,0:T(8,128)(2,1)} %get-tuple-element.110.keep, bf16[16,104,768]{2,1,0:T(8,128)(2,1)} %copy-done), custom_call_target="tpu_custom_call" | custom-call | flops 1277952 | bytes 7667712 | tf_op jit(solution)/shard_map/pair_sum/pallas_call | solution.py:634
  184.7 0.6 collective-permute-start.1
  185.3 1.5 collective-permute-start.12
  186.7 1.1 collective-permute-start.13
  187.9 1.5 collective-permute-start.2
  189.4 1.6 collective-permute-done.11.left
  191.0 1.5 collective-permute-start.3
  192.4 2.5 ring_sum.10
  195.0 7.9 %collective-permute-done.12.right = bf16[4,96,768]{2,1,0:T(8,128)(2,1)S(1)} collective-permute-done((bf16[4,96,768]{2,1,0:T(8,128)(2,1)}, bf16[4,96,768]{2,1,0:T(8,128)(2,1)S(1)}, u32[]{:S(2)}, u32[]{:S(2)}) %collective-permute-start.12) | collective-permute-done | bytes 589856 | tf_op jit(solution)/shard_map/ppermute | solution.py:638
  202.9 3.2 %collective-permute-start.25 = (bf16[96,768]{1,0:T(8,128)(2,1)}, bf16[96,768]{1,0:T(8,128)(2,1)S(1)}, u32[]{:S(2)}, u32[]{:S(2)}) collective-permute-start(bf16[96,768]{1,0:T(8,128)(2,1)} %get-tuple-element.146), channel_id=1, source_target_pairs={{0,6},{1,25},{2,0},{3,27},{4,2},{5,29},{6,4},{7,31},{8,14},{9,1},{... | collective-permute-start | bytes 442376 | tf_op jit(solution)/shard_map/ppermute | solution.py:644
  206.2 2.8 %ring_sum.8 = (bf16[96,768]{1,0:T(8,128)(2,1)}, bf16[96,768]{1,0:T(8,128)(2,1)}, bf16[96,768]{1,0:T(8,128)(2,1)}, bf16[96,768]{1,0:T(8,128)(2,1)}) custom-call(bf16[4,96,768]{2,1,0:T(8,128)(2,1)} %get-tuple-element.129.own, bf16[4,96,768]{2,1,0:T(8,128)(2,1)} %copy-done.6, bf16[4,96,768]{2,1,0:T(8,128)(2,1)} %copy-done.10, bf16[4,96,768]{2,1,0:T(8,128)(2,1)} %copy-done.11), custom_call_target="tpu_custom_call" | custom-call | flops 1179648 | bytes 2949120 | tf_op jit(solution)/shard_map/ring_sum/pallas_call | solution.py:640
  209.0 3.2 %collective-permute-done.2.right = bf16[4,104,768]{2,1,0:T(8,128)(2,1)S(1)} collective-permute-done((bf16[4,104,768]{2,1,0:T(8,128)(2,1)}, bf16[4,104,768]{2,1,0:T(8,128)(2,1)S(1)}, u32[]{:S(2)}, u32[]{:S(2)}) %collective-permute-start.2) | collective-permute-done | bytes 639008 | tf_op jit(solution)/shard_map/ppermute | solution.py:638
  212.1 0.8 collective-permute-start.14
  212.9 6.3 %collective-permute-done.3.far = bf16[4,104,768]{2,1,0:T(8,128)(2,1)S(1)} collective-permute-done((bf16[4,104,768]{2,1,0:T(8,128)(2,1)}, bf16[4,104,768]{2,1,0:T(8,128)(2,1)S(1)}, u32[]{:S(2)}, u32[]{:S(2)}) %collective-permute-start.3) | collective-permute-done | bytes 639008 | tf_op jit(solution)/shard_map/ppermute | solution.py:638
  219.2 0.8 copy-done.5
  220.1 2.6 ring_sum.6
  222.7 0.9 collective-permute-start.4
  223.6 2.3 collective-permute-start.5
  226.0 1.2 collective-permute-start.15
  227.1 0.7 collective-permute-start.16
  227.9 2.9 %collective-permute-start.6 = (bf16[104,768]{1,0:T(8,128)(2,1)}, bf16[104,768]{1,0:T(8,128)(2,1)S(1)}, u32[]{:S(2)}, u32[]{:S(2)}) collective-permute-start(bf16[104,768]{1,0:T(8,128)(2,1)} %get-tuple-element.119), channel_id=1, source_target_pairs={{0,4},{1,17},{2,6},{3,19},{4,0},{5,21},{6,2},{7,23},{8,12},{9,25},... | collective-permute-start | bytes 479240 | tf_op jit(solution)/shard_map/ppermute | solution.py:644
  230.8 1.9 ring_sum.11.own
  232.6 3.0 %collective-permute-start.29 = (bf16[96,768]{1,0:T(8,128)(2,1)}, bf16[96,768]{1,0:T(8,128)(2,1)S(1)}, u32[]{:S(2)}, u32[]{:S(2)}) collective-permute-start(bf16[96,768]{1,0:T(8,128)(2,1)} %ring_sum.11.own), channel_id=1, source_target_pairs={{0,64},{32,96},{64,0},{96,32},{1,65},{33,97},{65,1},{97,33},{2,66}... | collective-permute-start | bytes 442376 | tf_op jit(solution)/shard_map/ppermute | solution.py:649
  235.7 1.1 collective-permute-start.28
  236.8 1.8 ring_sum.9.own
  238.6 0.9 collective-permute-start.27
  239.5 1.2 collective-permute-start.19
  240.8 2.0 collective-permute-start.18
  242.8 1.9 ring_sum.7.own
  244.7 0.6 collective-permute-start.17
  245.3 1.7 collective-permute-start.9
  247.0 2.9 %collective-permute-done.27.left = bf16[96,768]{1,0:T(8,128)(2,1)S(1)} collective-permute-done((bf16[96,768]{1,0:T(8,128)(2,1)}, bf16[96,768]{1,0:T(8,128)(2,1)S(1)}, u32[]{:S(2)}, u32[]{:S(2)}) %collective-permute-start.27) | collective-permute-done | bytes 147488 | tf_op jit(solution)/shard_map/ppermute | solution.py:649
  250.0 2.0 collective-permute-start.7
  252.0 7.6 %input_back.1 = (f32[128,768]{1,0:T(8,128)}, f32[512,768]{1,0:T(8,128)}) custom-call(f32[640,768]{1,0:T(8,128)} %get-tuple-element.94.gfs, bf16[640,768]{1,0:T(8,128)(2,1)} %get-tuple-element.105.dq, bf16[640,768]{1,0:T(8,128)(2,1)} %get-tuple-element.106.dk, bf16[640,768]{1,0:T(8,128)(2,1)} %get-tuple-element.107.dv, bf16[32,296,768]{2,1,0:T(8,128)(2,1)} %bitcast.40, ...), custom_call_target="tpu_custom_call" | custom-call | flops 2264924160 | bytes 12000000 | tf_op jit(solution)/shard_map/input_back/pallas_call | solution.py:581
  259.6 1.9 finish_feed.3
  261.5 0.7 copy-done.22
  262.2 0.7 copy-done.23
  262.8 1.9 finish_feed.2
  264.8 0.6 copy-done.12
  265.4 0.1 copy-done.13
  265.5 0.7 copy-done.14
  266.1 1.9 finish_attention.1
  (82 shorter events, 0.2 us)
Async XLA Ops:
  7.2 73.7 %all-gather.3.cloned.1.call-start = ((), (), s32[]{:S(2)}) async-start(), calls=%async_computation | async-start | bytes 15003648 | tf_op jit(solution)/shard_map/all_gather | solution.py:721
  122.5 40.4 %collective-permute-start.20 = (bf16[16,96,768]{2,1,0:T(8,128)(2,1)}, bf16[16,96,768]{2,1,0:T(8,128)(2,1)S(1)}, u32[]{:S(2)}, u32[]{:S(2)}) collective-permute-start(bf16[16,96,768]{2,1,0:T(8,128)(2,1)} %get-tuple-element.139), channel_id=1, source_target_pairs={{0,1},{1,0},{2,3},{3,2},{4,5},{5,4},{6,7},{7,6},{8,9},{9,8},{10,11... | collective-permute-start | bytes 7077896 | tf_op jit(solution)/shard_map/ppermute | solution.py:627
  142.4 29.3 %collective-permute-start.10 = (bf16[16,96,768]{2,1,0:T(8,128)(2,1)}, bf16[16,96,768]{2,1,0:T(8,128)(2,1)S(1)}, u32[]{:S(2)}, u32[]{:S(2)}) collective-permute-start(bf16[16,96,768]{2,1,0:T(8,128)(2,1)} %get-tuple-element.128), channel_id=1, source_target_pairs={{0,1},{1,0},{2,3},{3,2},{4,5},{5,4},{6,7},{7,6},{8,9},{9,8},{10,11... | collective-permute-start | bytes 7077896 | tf_op jit(solution)/shard_map/ppermute | solution.py:627
  162.5 16.7 %collective-permute-start = (bf16[16,104,768]{2,1,0:T(8,128)(2,1)}, bf16[16,104,768]{2,1,0:T(8,128)(2,1)S(1)}, u32[]{:S(2)}, u32[]{:S(2)}) collective-permute-start(bf16[16,104,768]{2,1,0:T(8,128)(2,1)} %get-tuple-element.111), channel_id=1, source_target_pairs={{0,1},{1,0},{2,3},{3,2},{4,5},{5,4},{6,7},{7,6},{8,9},{9,8},{10,11... | collective-permute-start | bytes 7667720 | tf_op jit(solution)/shard_map/ppermute | solution.py:627
  162.8 1.4 copy-start.2
  168.2 17.1 %collective-permute-start.21 = (bf16[4,96,768]{2,1,0:T(8,128)(2,1)}, bf16[4,96,768]{2,1,0:T(8,128)(2,1)S(1)}, u32[]{:S(2)}, u32[]{:S(2)}) collective-permute-start(bf16[4,96,768]{2,1,0:T(8,128)(2,1)} %get-tuple-element.141), channel_id=1, source_target_pairs={{0,8},{1,3},{2,10},{3,5},{4,12},{5,7},{6,14},{7,1},{8,16},{9,11},{... | collective-permute-start | bytes 1769480 | tf_op jit(solution)/shard_map/ppermute | solution.py:638
  168.7 18.0 %collective-permute-start.22 = (bf16[4,96,768]{2,1,0:T(8,128)(2,1)}, bf16[4,96,768]{2,1,0:T(8,128)(2,1)S(1)}, u32[]{:S(2)}, u32[]{:S(2)}) collective-permute-start(bf16[4,96,768]{2,1,0:T(8,128)(2,1)} %get-tuple-element.142), channel_id=1, source_target_pairs={{0,24},{1,7},{2,26},{3,1},{4,28},{5,3},{6,30},{7,5},{8,0},{9,15},{... | collective-permute-start | bytes 1769480 | tf_op jit(solution)/shard_map/ppermute | solution.py:638
  170.2 17.7 %collective-permute-start.23 = (bf16[4,96,768]{2,1,0:T(8,128)(2,1)}, bf16[4,96,768]{2,1,0:T(8,128)(2,1)S(1)}, u32[]{:S(2)}, u32[]{:S(2)}) collective-permute-start(bf16[4,96,768]{2,1,0:T(8,128)(2,1)} %get-tuple-element.143), channel_id=1, source_target_pairs={{0,16},{1,5},{2,18},{3,7},{4,20},{5,1},{6,22},{7,3},{8,24},{9,13},... | collective-permute-start | bytes 1769480 | tf_op jit(solution)/shard_map/ppermute | solution.py:638
  171.7 1.4 copy-start.1
  177.1 13.9 %collective-permute-start.11 = (bf16[4,96,768]{2,1,0:T(8,128)(2,1)}, bf16[4,96,768]{2,1,0:T(8,128)(2,1)S(1)}, u32[]{:S(2)}, u32[]{:S(2)}) collective-permute-start(bf16[4,96,768]{2,1,0:T(8,128)(2,1)} %get-tuple-element.130), channel_id=1, source_target_pairs={{0,8},{1,3},{2,10},{3,5},{4,12},{5,7},{6,14},{7,1},{8,16},{9,11},{... | collective-permute-start | bytes 1769480 | tf_op jit(solution)/shard_map/ppermute | solution.py:638
  179.2 1.4 copy-start
  184.7 21.4 %collective-permute-start.1 = (bf16[4,104,768]{2,1,0:T(8,128)(2,1)}, bf16[4,104,768]{2,1,0:T(8,128)(2,1)S(1)}, u32[]{:S(2)}, u32[]{:S(2)}) collective-permute-start(bf16[4,104,768]{2,1,0:T(8,128)(2,1)} %get-tuple-element.113), channel_id=1, source_target_pairs={{0,8},{1,3},{2,10},{3,5},{4,12},{5,7},{6,14},{7,1},{8,16},{9,11},{... | collective-permute-start | bytes 1916936 | tf_op jit(solution)/shard_map/ppermute | solution.py:638
  185.3 7.2 %copy-start.7 = (bf16[4,96,768]{2,1,0:T(8,128)(2,1)}, bf16[4,96,768]{2,1,0:T(8,128)(2,1)S(1)}, u32[]{:S(2)}) copy-start(bf16[4,96,768]{2,1,0:T(8,128)(2,1)S(1)} %collective-permute-done.21.left) | copy-start | bytes 1769476
  185.3 17.6 %collective-permute-start.12 = (bf16[4,96,768]{2,1,0:T(8,128)(2,1)}, bf16[4,96,768]{2,1,0:T(8,128)(2,1)S(1)}, u32[]{:S(2)}, u32[]{:S(2)}) collective-permute-start(bf16[4,96,768]{2,1,0:T(8,128)(2,1)} %get-tuple-element.131), channel_id=1, source_target_pairs={{0,24},{1,7},{2,26},{3,1},{4,28},{5,3},{6,30},{7,5},{8,0},{9,15},{... | collective-permute-start | bytes 1769480 | tf_op jit(solution)/shard_map/ppermute | solution.py:638
  186.7 5.7 %copy-start.8 = (bf16[4,96,768]{2,1,0:T(8,128)(2,1)}, bf16[4,96,768]{2,1,0:T(8,128)(2,1)S(1)}, u32[]{:S(2)}) copy-start(bf16[4,96,768]{2,1,0:T(8,128)(2,1)S(1)} %collective-permute-done.22.right) | copy-start | bytes 1769476
  186.7 16.2 %collective-permute-start.13 = (bf16[4,96,768]{2,1,0:T(8,128)(2,1)}, bf16[4,96,768]{2,1,0:T(8,128)(2,1)S(1)}, u32[]{:S(2)}, u32[]{:S(2)}) collective-permute-start(bf16[4,96,768]{2,1,0:T(8,128)(2,1)} %get-tuple-element.132), channel_id=1, source_target_pairs={{0,16},{1,5},{2,18},{3,7},{4,20},{5,1},{6,22},{7,3},{8,24},{9,13},... | collective-permute-start | bytes 1769480 | tf_op jit(solution)/shard_map/ppermute | solution.py:638
  187.9 4.6 %copy-start.9 = (bf16[4,96,768]{2,1,0:T(8,128)(2,1)}, bf16[4,96,768]{2,1,0:T(8,128)(2,1)S(1)}, u32[]{:S(2)}) copy-start(bf16[4,96,768]{2,1,0:T(8,128)(2,1)S(1)} %collective-permute-done.23.far) | copy-start | bytes 1769476
  187.9 24.2 %collective-permute-start.2 = (bf16[4,104,768]{2,1,0:T(8,128)(2,1)}, bf16[4,104,768]{2,1,0:T(8,128)(2,1)S(1)}, u32[]{:S(2)}, u32[]{:S(2)}) collective-permute-start(bf16[4,104,768]{2,1,0:T(8,128)(2,1)} %get-tuple-element.114), channel_id=1, source_target_pairs={{0,24},{1,7},{2,26},{3,1},{4,28},{5,3},{6,30},{7,5},{8,0},{9,15},{... | collective-permute-start | bytes 1916936 | tf_op jit(solution)/shard_map/ppermute | solution.py:638
  191.0 15.2 %copy-start.6 = (bf16[4,96,768]{2,1,0:T(8,128)(2,1)}, bf16[4,96,768]{2,1,0:T(8,128)(2,1)S(1)}, u32[]{:S(2)}) copy-start(bf16[4,96,768]{2,1,0:T(8,128)(2,1)S(1)} %collective-permute-done.11.left) | copy-start | bytes 1769476
  191.0 28.2 %collective-permute-start.3 = (bf16[4,104,768]{2,1,0:T(8,128)(2,1)}, bf16[4,104,768]{2,1,0:T(8,128)(2,1)S(1)}, u32[]{:S(2)}, u32[]{:S(2)}) collective-permute-start(bf16[4,104,768]{2,1,0:T(8,128)(2,1)} %get-tuple-element.115), channel_id=1, source_target_pairs={{0,16},{1,5},{2,18},{3,7},{4,20},{5,1},{6,22},{7,3},{8,24},{9,13},... | collective-permute-start | bytes 1916936 | tf_op jit(solution)/shard_map/ppermute | solution.py:638
  202.9 3.3 %copy-start.10 = (bf16[4,96,768]{2,1,0:T(8,128)(2,1)}, bf16[4,96,768]{2,1,0:T(8,128)(2,1)S(1)}, u32[]{:S(2)}) copy-start(bf16[4,96,768]{2,1,0:T(8,128)(2,1)S(1)} %collective-permute-done.12.right) | copy-start | bytes 1769476
  202.9 20.7 %collective-permute-start.24 = (bf16[96,768]{1,0:T(8,128)(2,1)}, bf16[96,768]{1,0:T(8,128)(2,1)S(1)}, u32[]{:S(2)}, u32[]{:S(2)}) collective-permute-start(bf16[96,768]{1,0:T(8,128)(2,1)} %get-tuple-element.145), channel_id=1, source_target_pairs={{0,2},{1,9},{2,4},{3,11},{4,6},{5,13},{6,0},{7,15},{8,10},{9,17},{... | collective-permute-start | bytes 442376 | tf_op jit(solution)/shard_map/ppermute | solution.py:644
  202.9 3.3 %copy-start.11 = (bf16[4,96,768]{2,1,0:T(8,128)(2,1)}, bf16[4,96,768]{2,1,0:T(8,128)(2,1)S(1)}, u32[]{:S(2)}) copy-start(bf16[4,96,768]{2,1,0:T(8,128)(2,1)S(1)} %collective-permute-done.13.far) | copy-start | bytes 1769476
  202.9 23.0 %collective-permute-start.25 = (bf16[96,768]{1,0:T(8,128)(2,1)}, bf16[96,768]{1,0:T(8,128)(2,1)S(1)}, u32[]{:S(2)}, u32[]{:S(2)}) collective-permute-start(bf16[96,768]{1,0:T(8,128)(2,1)} %get-tuple-element.146), channel_id=1, source_target_pairs={{0,6},{1,25},{2,0},{3,27},{4,2},{5,29},{6,4},{7,31},{8,14},{9,1},{... | collective-permute-start | bytes 442376 | tf_op jit(solution)/shard_map/ppermute | solution.py:644
  206.1 13.1 %copy-start.3 = (bf16[4,104,768]{2,1,0:T(8,128)(2,1)}, bf16[4,104,768]{2,1,0:T(8,128)(2,1)S(1)}, u32[]{:S(2)}) copy-start(bf16[4,104,768]{2,1,0:T(8,128)(2,1)S(1)} %collective-permute-done.1.left) | copy-start | bytes 1916932
  206.1 21.0 %collective-permute-start.26 = (bf16[96,768]{1,0:T(8,128)(2,1)}, bf16[96,768]{1,0:T(8,128)(2,1)S(1)}, u32[]{:S(2)}, u32[]{:S(2)}) collective-permute-start(bf16[96,768]{1,0:T(8,128)(2,1)} %get-tuple-element.147), channel_id=1, source_target_pairs={{0,4},{1,17},{2,6},{3,19},{4,0},{5,21},{6,2},{7,23},{8,12},{9,25},... | collective-permute-start | bytes 442376 | tf_op jit(solution)/shard_map/ppermute | solution.py:644
  208.9 17.0 %copy-start.31 = (bf16[96,768]{1,0:T(8,128)(2,1)S(1)}, bf16[96,768]{1,0:T(8,128)(2,1)}, u32[]{:S(2)}) copy-start(bf16[96,768]{1,0:T(8,128)(2,1)} %get-tuple-element.135) | copy-start | bytes 442372
  208.9 18.2 %copy-start.30 = (bf16[96,768]{1,0:T(8,128)(2,1)S(1)}, bf16[96,768]{1,0:T(8,128)(2,1)}, u32[]{:S(2)}) copy-start(bf16[96,768]{1,0:T(8,128)(2,1)} %get-tuple-element.136) | copy-start | bytes 442372
  212.1 7.1 %copy-start.4 = (bf16[4,104,768]{2,1,0:T(8,128)(2,1)}, bf16[4,104,768]{2,1,0:T(8,128)(2,1)S(1)}, u32[]{:S(2)}) copy-start(bf16[4,104,768]{2,1,0:T(8,128)(2,1)S(1)} %collective-permute-done.2.right) | copy-start | bytes 1916932
  212.1 15.8 %collective-permute-start.14 = (bf16[96,768]{1,0:T(8,128)(2,1)}, bf16[96,768]{1,0:T(8,128)(2,1)S(1)}, u32[]{:S(2)}, u32[]{:S(2)}) collective-permute-start(bf16[96,768]{1,0:T(8,128)(2,1)} %get-tuple-element.134), channel_id=1, source_target_pairs={{0,2},{1,9},{2,4},{3,11},{4,6},{5,13},{6,0},{7,15},{8,10},{9,17},{... | collective-permute-start | bytes 442376 | tf_op jit(solution)/shard_map/ppermute | solution.py:644
  219.2 0.8 copy-start.5
  222.7 15.9 %collective-permute-start.4 = (bf16[104,768]{1,0:T(8,128)(2,1)}, bf16[104,768]{1,0:T(8,128)(2,1)S(1)}, u32[]{:S(2)}, u32[]{:S(2)}) collective-permute-start(bf16[104,768]{1,0:T(8,128)(2,1)} %get-tuple-element.117), channel_id=1, source_target_pairs={{0,2},{1,9},{2,4},{3,11},{4,6},{5,13},{6,0},{7,15},{8,10},{9,17},{... | collective-permute-start | bytes 479240 | tf_op jit(solution)/shard_map/ppermute | solution.py:644
  223.6 7.1 %copy-start.24 = (bf16[96,768]{1,0:T(8,128)(2,1)}, bf16[96,768]{1,0:T(8,128)(2,1)S(1)}, u32[]{:S(2)}) copy-start(bf16[96,768]{1,0:T(8,128)(2,1)S(1)} %collective-permute-done.24.left) | copy-start | bytes 442372
  223.6 15.9 %collective-permute-start.5 = (bf16[104,768]{1,0:T(8,128)(2,1)}, bf16[104,768]{1,0:T(8,128)(2,1)S(1)}, u32[]{:S(2)}, u32[]{:S(2)}) collective-permute-start(bf16[104,768]{1,0:T(8,128)(2,1)} %get-tuple-element.118), channel_id=1, source_target_pairs={{0,6},{1,25},{2,0},{3,27},{4,2},{5,29},{6,4},{7,31},{8,14},{9,1},{... | collective-permute-start | bytes 479240 | tf_op jit(solution)/shard_map/ppermute | solution.py:644
  225.9 4.8 %copy-start.25 = (bf16[96,768]{1,0:T(8,128)(2,1)}, bf16[96,768]{1,0:T(8,128)(2,1)S(1)}, u32[]{:S(2)}) copy-start(bf16[96,768]{1,0:T(8,128)(2,1)S(1)} %collective-permute-done.25.right) | copy-start | bytes 442372
  226.0 6.7 %collective-permute-start.15 = (bf16[96,768]{1,0:T(8,128)(2,1)S(1)}, bf16[96,768]{1,0:T(8,128)(2,1)S(1)}, u32[]{:S(2)}, u32[]{:S(2)}) collective-permute-start(bf16[96,768]{1,0:T(8,128)(2,1)S(1)} %copy-done.31), channel_id=1, source_target_pairs={{0,6},{1,25},{2,0},{3,27},{4,2},{5,29},{6,4},{7,31},{8,14},{9,1},{... | collective-permute-start | bytes 442376 | tf_op jit(solution)/shard_map/ppermute | solution.py:644
  227.1 3.6 %copy-start.27 = (bf16[96,768]{1,0:T(8,128)(2,1)}, bf16[96,768]{1,0:T(8,128)(2,1)S(1)}, u32[]{:S(2)}) copy-start(bf16[96,768]{1,0:T(8,128)(2,1)S(1)} %collective-permute-done.26.far) | copy-start | bytes 442372
  227.1 8.5 %collective-permute-start.16 = (bf16[96,768]{1,0:T(8,128)(2,1)S(1)}, bf16[96,768]{1,0:T(8,128)(2,1)S(1)}, u32[]{:S(2)}, u32[]{:S(2)}) collective-permute-start(bf16[96,768]{1,0:T(8,128)(2,1)S(1)} %copy-done.30), channel_id=1, source_target_pairs={{0,4},{1,17},{2,6},{3,19},{4,0},{5,21},{6,2},{7,23},{8,12},{9,25},... | collective-permute-start | bytes 442376 | tf_op jit(solution)/shard_map/ppermute | solution.py:644
  227.9 8.9 %copy-start.26 = (bf16[96,768]{1,0:T(8,128)(2,1)}, bf16[96,768]{1,0:T(8,128)(2,1)S(1)}, u32[]{:S(2)}) copy-start(bf16[96,768]{1,0:T(8,128)(2,1)S(1)} %collective-permute-done.14.left) | copy-start | bytes 442372
  227.9 12.9 %collective-permute-start.6 = (bf16[104,768]{1,0:T(8,128)(2,1)}, bf16[104,768]{1,0:T(8,128)(2,1)S(1)}, u32[]{:S(2)}, u32[]{:S(2)}) collective-permute-start(bf16[104,768]{1,0:T(8,128)(2,1)} %get-tuple-element.119), channel_id=1, source_target_pairs={{0,4},{1,17},{2,6},{3,19},{4,0},{5,21},{6,2},{7,23},{8,12},{9,25},... | collective-permute-start | bytes 479240 | tf_op jit(solution)/shard_map/ppermute | solution.py:644
  232.6 4.2 %copy-start.28 = (bf16[96,768]{1,0:T(8,128)(2,1)}, bf16[96,768]{1,0:T(8,128)(2,1)S(1)}, u32[]{:S(2)}) copy-start(bf16[96,768]{1,0:T(8,128)(2,1)S(1)} %collective-permute-done.15.right) | copy-start | bytes 442372
  232.6 12.1 %collective-permute-start.29 = (bf16[96,768]{1,0:T(8,128)(2,1)}, bf16[96,768]{1,0:T(8,128)(2,1)S(1)}, u32[]{:S(2)}, u32[]{:S(2)}) collective-permute-start(bf16[96,768]{1,0:T(8,128)(2,1)} %ring_sum.11.own), channel_id=1, source_target_pairs={{0,64},{32,96},{64,0},{96,32},{1,65},{33,97},{65,1},{97,33},{2,66}... | collective-permute-start | bytes 442376 | tf_op jit(solution)/shard_map/ppermute | solution.py:649
  235.6 1.1 copy-start.29
  235.7 9.7 %collective-permute-start.28 = (bf16[96,768]{1,0:T(8,128)(2,1)}, bf16[96,768]{1,0:T(8,128)(2,1)S(1)}, u32[]{:S(2)}, u32[]{:S(2)}) collective-permute-start(bf16[96,768]{1,0:T(8,128)(2,1)} %ring_sum.11.own), channel_id=1, source_target_pairs={{0,96},{32,0},{64,32},{96,64},{1,97},{33,1},{65,33},{97,65},{2,98}... | collective-permute-start | bytes 442376 | tf_op jit(solution)/shard_map/ppermute | solution.py:649
  238.6 4.2 %copy-start.15 = (bf16[104,768]{1,0:T(8,128)(2,1)}, bf16[104,768]{1,0:T(8,128)(2,1)S(1)}, u32[]{:S(2)}) copy-start(bf16[104,768]{1,0:T(8,128)(2,1)S(1)} %collective-permute-done.4.left) | copy-start | bytes 479236
  238.6 11.3 %collective-permute-start.27 = (bf16[96,768]{1,0:T(8,128)(2,1)}, bf16[96,768]{1,0:T(8,128)(2,1)S(1)}, u32[]{:S(2)}, u32[]{:S(2)}) collective-permute-start(bf16[96,768]{1,0:T(8,128)(2,1)} %ring_sum.11.own), channel_id=1, source_target_pairs={{0,32},{32,64},{64,96},{96,0},{1,33},{33,65},{65,97},{97,1},{2,34}... | collective-permute-start | bytes 442376 | tf_op jit(solution)/shard_map/ppermute | solution.py:649
  239.5 3.3 %copy-start.16 = (bf16[104,768]{1,0:T(8,128)(2,1)}, bf16[104,768]{1,0:T(8,128)(2,1)S(1)}, u32[]{:S(2)}) copy-start(bf16[104,768]{1,0:T(8,128)(2,1)S(1)} %collective-permute-done.5.right) | copy-start | bytes 479236
  239.5 10.4 %collective-permute-start.19 = (bf16[96,768]{1,0:T(8,128)(2,1)}, bf16[96,768]{1,0:T(8,128)(2,1)S(1)}, u32[]{:S(2)}, u32[]{:S(2)}) collective-permute-start(bf16[96,768]{1,0:T(8,128)(2,1)} %ring_sum.9.own), channel_id=1, source_target_pairs={{0,64},{32,96},{64,0},{96,32},{1,65},{33,97},{65,1},{97,33},{2,66}... | collective-permute-start | bytes 442376 | tf_op jit(solution)/shard_map/ppermute | solution.py:649
  240.8 2.0 copy-start.17
  240.8 20.7 %collective-permute-start.18 = (bf16[96,768]{1,0:T(8,128)(2,1)}, bf16[96,768]{1,0:T(8,128)(2,1)S(1)}, u32[]{:S(2)}, u32[]{:S(2)}) collective-permute-start(bf16[96,768]{1,0:T(8,128)(2,1)} %ring_sum.9.own), channel_id=1, source_target_pairs={{0,96},{32,0},{64,32},{96,64},{1,97},{33,1},{65,33},{97,65},{2,98}... | collective-permute-start | bytes 442376 | tf_op jit(solution)/shard_map/ppermute | solution.py:649
  244.7 14.9 %copy-start.18 = (bf16[96,768]{1,0:T(8,128)(2,1)}, bf16[96,768]{1,0:T(8,128)(2,1)S(1)}, u32[]{:S(2)}) copy-start(bf16[96,768]{1,0:T(8,128)(2,1)S(1)} %collective-permute-done.29.far) | copy-start | bytes 442372
  244.7 16.8 %collective-permute-start.17 = (bf16[96,768]{1,0:T(8,128)(2,1)}, bf16[96,768]{1,0:T(8,128)(2,1)S(1)}, u32[]{:S(2)}, u32[]{:S(2)}) collective-permute-start(bf16[96,768]{1,0:T(8,128)(2,1)} %ring_sum.9.own), channel_id=1, source_target_pairs={{0,32},{32,64},{64,96},{96,0},{1,33},{33,65},{65,97},{97,1},{2,34}... | collective-permute-start | bytes 442376 | tf_op jit(solution)/shard_map/ppermute | solution.py:649
  245.3 14.2 %copy-start.19 = (bf16[96,768]{1,0:T(8,128)(2,1)}, bf16[96,768]{1,0:T(8,128)(2,1)S(1)}, u32[]{:S(2)}) copy-start(bf16[96,768]{1,0:T(8,128)(2,1)S(1)} %collective-permute-done.28.right) | copy-start | bytes 442372
  245.3 19.4 %collective-permute-start.9 = (bf16[104,768]{1,0:T(8,128)(2,1)}, bf16[104,768]{1,0:T(8,128)(2,1)S(1)}, u32[]{:S(2)}, u32[]{:S(2)}) collective-permute-start(bf16[104,768]{1,0:T(8,128)(2,1)} %ring_sum.7.own), channel_id=1, source_target_pairs={{0,64},{32,96},{64,0},{96,32},{1,65},{33,97},{65,1},{97,33},{2,66}... | collective-permute-start | bytes 479240 | tf_op jit(solution)/shard_map/ppermute | solution.py:649
  250.0 9.6 %copy-start.21 = (bf16[96,768]{1,0:T(8,128)(2,1)}, bf16[96,768]{1,0:T(8,128)(2,1)S(1)}, u32[]{:S(2)}) copy-start(bf16[96,768]{1,0:T(8,128)(2,1)S(1)} %collective-permute-done.27.left) | copy-start | bytes 442372
  250.0 14.8 %collective-permute-start.8 = (bf16[104,768]{1,0:T(8,128)(2,1)}, bf16[104,768]{1,0:T(8,128)(2,1)S(1)}, u32[]{:S(2)}, u32[]{:S(2)}) collective-permute-start(bf16[104,768]{1,0:T(8,128)(2,1)} %ring_sum.7.own), channel_id=1, source_target_pairs={{0,96},{32,0},{64,32},{96,64},{1,97},{33,1},{65,33},{97,65},{2,98}... | collective-permute-start | bytes 479240 | tf_op jit(solution)/shard_map/ppermute | solution.py:649
  250.0 9.6 %copy-start.20 = (bf16[96,768]{1,0:T(8,128)(2,1)}, bf16[96,768]{1,0:T(8,128)(2,1)S(1)}, u32[]{:S(2)}) copy-start(bf16[96,768]{1,0:T(8,128)(2,1)S(1)} %collective-permute-done.19.far) | copy-start | bytes 442372
  250.0 14.8 %collective-permute-start.7 = (bf16[104,768]{1,0:T(8,128)(2,1)}, bf16[104,768]{1,0:T(8,128)(2,1)S(1)}, u32[]{:S(2)}, u32[]{:S(2)}) collective-permute-start(bf16[104,768]{1,0:T(8,128)(2,1)} %ring_sum.7.own), channel_id=1, source_target_pairs={{0,32},{32,64},{64,96},{96,0},{1,33},{33,65},{65,97},{97,1},{2,34}... | collective-permute-start | bytes 479240 | tf_op jit(solution)/shard_map/ppermute | solution.py:649
  261.5 0.7 copy-start.22
  262.2 0.7 copy-start.23
  264.7 0.7 copy-start.12
  264.7 0.7 copy-start.13
  265.5 0.7 copy-start.14
Sparse Core Ops, SparseCore 0:
  10.9 69.9 all-gather.2
